TPU v7x, 256 devices: a whole 4x4x8 slice. The times are simulated.
256 devices in a mesh: scen: 4 (over y), fac: 64 (over z, x, core).
Axes of the slice: x: 4, y: 4, z: 8, core: 2. Of those that a mesh axis runs over, the one named last changes fastest.
Arguments:
- loadings: bfloat16 [65536, 1000], P('fac'), may hold values from -0.1875 to 0.1875
- reduced_shocks: bfloat16 [1000, 256], P(None, 'scen'), may hold values from -6 to 6
- sensitivity: bfloat16 [65536, 200], P('fac'), may hold values from -0.0234375 to 0.0234375
- cross_gamma: bfloat16 [128, 1024, 1024], P('fac'), may hold values from -0.005859375 to 0.005859375
- block_list: int32 [96, 3], replicated, may hold values from 0 to 199, as said below
- block_owner: int32 [96], replicated, may hold values from 0 to 63, as said below
- desk_owner: int32 [200], replicated, may hold values from 0 to 63, as said below
- buckets: int32 [65536], replicated, may hold values from 0 to 4
Outputs:
- desk_profit: float32 [320, 5, 256], P('fac', None, 'scen')
- shortfall: float32 [320, 5], P('fac')
- adjusted_es: float32 [320], P('fac')
Inputs may be any that keep to these rules, and one draw needn't show every extreme that they name: `block_list`: each row is (row block, column block, desk): block numbers below 64, desks below 200; the fac index holding the row block, and the one holding the column block, is at most two away from the block's owner. `block_owner`: no fac index owns more than 2 blocks; some index owns exactly 2. `desk_owner`: no fac index owns more than 5 desks; some index owns exactly 5.
All inputs are finite; a program needn't handle non-finite values.
Results may differ from a plain program's by a relative error of at most 0.0032.
Values may be sent and summed in bfloat16 or wider, within the bound.
No kernel may reach another device: no remote copies, remote signals or barrier semaphores. Data moves between devices by JAX's collectives and lax.ppermute only.
A program may use at most 64 MiB of HBM per device.

v0:
```python
import jax
import jax.numpy as jnp
from jax import lax
from jax.sharding import PartitionSpec as P

BLK = 1024
HORIZONS = 5
CAP = 2


horizon_weights = (1.0, 1.0, 2.0, 2.0, 6.0)


def passed_along(value, axis, steps):
    count = lax.axis_size(axis)
    initial, last = (max(0, -steps), min(count, count - steps))
    return lax.ppermute(value, axis, [(source, source + steps) for source in range(initial, last)])


def owner_ranks(owners):
    position = jnp.arange(owners.shape[0], dtype=jnp.int32)
    same_owner = owners[:, None] == owners[None, :]
    earlier = position[None, :] < position[:, None]
    return jnp.sum((same_owner & earlier).astype(jnp.int32), axis=1)


def apply_masks(shocks, bucket_ids):
    horizon = jnp.arange(HORIZONS, dtype=jnp.int32)
    keeps_factor = bucket_ids[:, None] >= horizon[None, :]
    masked = jnp.where(keeps_factor[:, :, None], shocks[:, None, :], jnp.zeros((), jnp.bfloat16))
    return masked.reshape(shocks.shape[0], HORIZONS * shocks.shape[1])


def local(
    loadings, reduced_shocks, sensitivity, cross_gamma, block_list, block_owner, desk_owner, buckets
):
    device = lax.axis_index("fac")
    fac_count = lax.axis_size("fac")
    f_dev = loadings.shape[0]
    s_dev = reduced_shocks.shape[1]
    desks = sensitivity.shape[1]
    blocks = block_owner.shape[0]
    shocks = jnp.dot(loadings, reduced_shocks, preferred_element_type=jnp.float32).astype(
        jnp.bfloat16
    )
    own_buckets = lax.dynamic_slice_in_dim(buckets, device * f_dev, f_dev)
    masked = apply_masks(shocks, own_buckets)
    partial_value = lax.dot_general(
        sensitivity, masked, (((0,), (0,)), ((), ())), preferred_element_type=jnp.float32
    )
    pieces = {}
    for distance in (2, 1, -1, -2):
        pieces[distance] = passed_along(masked, "fac", distance)
    window = jnp.concatenate([pieces[2], pieces[1], masked, pieces[-1], pieces[-2]], axis=0)
    row_base = (device - 2) * f_dev
    block_rank = owner_ranks(block_owner)
    owned = block_owner == device
    slot_ids = jnp.arange(CAP, dtype=jnp.int32)
    picked = owned[None, :] & (block_rank[None, :] == slot_ids[:, None])
    slot_block = jnp.sum(jnp.where(picked, jnp.arange(blocks, dtype=jnp.int32)[None, :], 0), axis=1)
    live_blocks = jnp.sum(owned.astype(jnp.int32))
    desk_ids = jnp.arange(desks, dtype=jnp.int32)

    def add_block(slot_index, running):
        block_entry = block_list[slot_block[slot_index]]
        matrix = lax.dynamic_index_in_dim(cross_gamma, slot_index, 0, keepdims=False)
        row_part = lax.dynamic_slice_in_dim(window, block_entry[0] * BLK - row_base, BLK, 0)
        col_part = lax.dynamic_slice_in_dim(window, block_entry[1] * BLK - row_base, BLK, 0)
        product = jnp.dot(matrix, col_part, preferred_element_type=jnp.float32)
        quad_term = 0.5 * jnp.sum(row_part.astype(jnp.float32) * product, axis=0)
        return running + jnp.where(
            (desk_ids == block_entry[2])[:, None], quad_term[None, :], jnp.zeros((), jnp.float32)
        )

    partial_value = lax.fori_loop(0, live_blocks, add_block, partial_value)
    desk_dev = (desks + fac_count - 1) // fac_count + 1
    desk_slot = desk_owner * desk_dev + owner_ranks(desk_owner)
    placement = (
        desk_slot[:, None] == jnp.arange(desk_dev * fac_count, dtype=jnp.int32)[None, :]
    ).astype(jnp.float32)
    desk_terms = lax.dot_general(
        placement,
        partial_value,
        (((0,), (0,)), ((), ())),
        precision=lax.Precision.HIGHEST,
        preferred_element_type=jnp.float32,
    )
    owned_rows = lax.psum_scatter(desk_terms, "fac", scatter_dimension=0, tiled=True)
    profit = owned_rows.reshape(desk_dev, HORIZONS, s_dev)
    tail_count = (s_dev * lax.axis_size("scen") * 25 + 999) // 1000
    all_scenarios = lax.all_gather(profit, "scen", axis=2, tiled=True)
    worst_losses = lax.top_k(-all_scenarios, tail_count)[0]
    shortfall = jnp.mean(worst_losses, axis=2)
    weights = jnp.array(horizon_weights, jnp.float32)
    adjusted = jnp.sqrt(jnp.sum(weights[None, :] * shortfall * shortfall, axis=1) + 1e-06)
    return (profit, shortfall, adjusted)


def solution(mesh):
    return jax.shard_map(
        local,
        mesh=mesh,
        in_specs=(
            P("fac", None),
            P(None, "scen"),
            P("fac", None),
            P("fac", None, None),
            P(),
            P(),
            P(),
            P(),
        ),
        out_specs=(P("fac", None, "scen"), P("fac", None), P("fac")),
        check_vma=False,
    )
```

profile of v0, /device:TPU:2, one launch (start us, length us, event | category | flops | bytes accessed | tf_op | source)
XLA Modules:
  0.0 280.5 jit_solution(8512004316310504553)
XLA Ops:
  7.2 0.0 copy-start
  7.2 0.0 all-reduce.3.cloned.1.call-start
  7.3 0.8 dynamic_slice.19
  8.1 0.6 copy-done
  8.8 1.4 convolution_convert_fusion
  10.1 0.1 broadcast_select_fusion
  10.2 3.4 %collective-permute-start = (bf16[1024,320]{0,1:T(8,128)(2,1)S(1)}, bf16[1024,320]{0,1:T(8,128)(2,1)}, u32[]{:S(2)}, u32[]{:S(2)}) collective-permute-start(bf16[1024,320]{0,1:T(8,128)(2,1)S(1)} %bitcast.30), channel_id=1, source_target_pairs={{0,2},{1,3},{2,4},{3,5},{4,6},{5,7},{6,8},{7,9},{8,10},{9,11},{10,... | collective-permute-start | bytes 1966088 | tf_op jit(solution)/shard_map/ppermute | solution.py:17
  13.6 1.9 collective-permute-start.1
  15.5 3.6 %collective-permute-start.2 = (bf16[1024,320]{0,1:T(8,128)(2,1)S(1)}, bf16[1024,320]{0,1:T(8,128)(2,1)}, u32[]{:S(2)}, u32[]{:S(2)}) collective-permute-start(bf16[1024,320]{0,1:T(8,128)(2,1)S(1)} %bitcast.32), channel_id=1, source_target_pairs={{1,0},{2,1},{3,2},{4,3},{5,4},{6,5},{7,6},{8,7},{9,8},{10,9},{11,1... | collective-permute-start | bytes 1966088 | tf_op jit(solution)/shard_map/ppermute | solution.py:17
  19.2 1.9 collective-permute-start.3
  21.1 0.4 convolution_bitcast_fusion
  21.6 0.0 copy-done.5
  21.6 0.2 convert_reduce_fusion
  21.8 0.6 convert_reduce_fusion.2
  22.4 0.2 convert_reduce_fusion.1
  22.6 0.1 fusion.17
  22.7 0.0 copy-start.4
  22.7 7.1 %collective-permute-done = bf16[1024,320]{0,1:T(8,128)(2,1)} collective-permute-done((bf16[1024,320]{0,1:T(8,128)(2,1)S(1)}, bf16[1024,320]{0,1:T(8,128)(2,1)}, u32[]{:S(2)}, u32[]{:S(2)}) %collective-permute-start) | collective-permute-done | bytes 655392 | tf_op jit(solution)/shard_map/ppermute | solution.py:17
  29.8 1.1 constant_dynamic-update-slice_fusion.4
  30.9 4.8 %collective-permute-done.1 = bf16[1024,320]{0,1:T(8,128)(2,1)} collective-permute-done((bf16[1024,320]{0,1:T(8,128)(2,1)S(1)}, bf16[1024,320]{0,1:T(8,128)(2,1)}, u32[]{:S(2)}, u32[]{:S(2)}) %collective-permute-start.1) | collective-permute-done | bytes 655392 | tf_op jit(solution)/shard_map/ppermute | solution.py:17
  35.7 1.1 constant_dynamic-update-slice_fusion.3
  36.9 0.0 collective-permute-done.2
  36.9 1.1 constant_dynamic-update-slice_fusion.1
  38.0 5.0 %collective-permute-done.3 = bf16[1024,320]{0,1:T(8,128)(2,1)} collective-permute-done((bf16[1024,320]{0,1:T(8,128)(2,1)S(1)}, bf16[1024,320]{0,1:T(8,128)(2,1)}, u32[]{:S(2)}, u32[]{:S(2)}) %collective-permute-start.3) | collective-permute-done | bytes 655392 | tf_op jit(solution)/shard_map/ppermute | solution.py:17
  43.1 1.1 constant_dynamic-update-slice_fusion
  44.2 1.7 copy-done.2
  45.9 9.1 %while.11 = (s32[]{:T(128)}, f32[200,320]{1,0:T(8,128)S(1)}, s32[]{:T(128)}, s32[2]{0:T(128)S(1)}, s32[96,3]{0,1:T(4,128)S(1)}, /*index=5*/s32[]{:T(128)}, bf16[...) while((s32[]{:T(128)}, f32[200,320]{1,0:T(8,128)S(1)}, ...), condition=%wide.region_6.7_spmd.clone, body=%wide.region_4.6_spmd.clone.sunk | while | flops 672199872 | bytes 3925789 | solution.py:75
  46.6 0.6 dynamic_slice.46
  48.9 0.1 constant_dynamic-slice_fusion.3
  48.9 0.6 fusion.30
  50.8 2.9 %fusion.31 = f32[320]{0:T(512)S(1)} fusion(bf16[2,1024,1024]{2,1,0:T(8,128)(2,1)} %get-tuple-element.195, s32[]{:T(128)S(6)} %select_n.53, bf16[5120,320]{0,1:T(8,128)(2,1)} %get-tuple-element.194, s32[]{:T(128)S(6)} %select_n.55, s32[]{:T(128)S(6)} %select_n.56), kind=kOutput, calls=%fused_computation.5.clone.1 | convolution fusion | flops 672071360 | bytes 3409164 | tf_op jit(solution)/shard_map/while/body/dot_general | solution.py:69
  53.7 0.6 iota_compare_fusion.7
  54.3 0.1 select_add_fusion.2
  55.1 0.0 copy-start.6
  55.1 1.4 fusion.13
  56.5 0.0 all-reduce.3.cloned.1.call-update
  56.5 0.6 dynamic-slice
  57.7 194.5 %all-reduce.3.cloned.1.call-done = f32[320,320]{1,0:T(8,128)} async-done(((f32[320,320]{1,0:T(8,128)}), f32[320,320]{1,0:T(8,128)}) %all-reduce.3.cloned.1.call-update) | async-done | bytes 409616
  252.2 0.7 constant_dynamic-slice_fusion.1
  253.0 0.1 reshape.60
  253.1 0.2 copy.18
  253.2 15.0 %all_gather.3 = f32[5,5,256]{1,0,2:T(8,128)S(1)} all-gather(f32[5,5,64]{1,0,2:T(8,128)S(1)} %copy.18), channel_id=1, replica_groups=mesh['scen'=4,'fac'=64] {'scen'}, dimensions={2}, use_global_device_ids=true | all-gather | bytes 32000 | tf_op jit(solution)/shard_map/all_gather | solution.py:91
  268.3 0.4 copy.19
  268.7 3.6 %sort_prefixfusion = f32[5,5,7]{2,0,1:T(8,128)S(1)} fusion(f32[5,5,256]{2,0,1:T(8,128)S(1)} %neg.3), kind=kCustom, calls=%top_k.9.sort_prefix | custom fusion | flops 83200 | bytes 26300 | tf_op jit(solution)/shard_map/top_k | solution.py:92
  272.2 0.1 reduce_sum.67
  272.3 0.1 multiply_reduce_fusion
  272.4 0.7 copy.20
  273.1 0.5 add_sqrt_fusion
  (17 shorter events, 0.1 us)
Async XLA Ops:
  7.2 1.6 copy-start
  7.2 13.9 %copy-start.1 = (bf16[1024,200]{0,1:T(8,128)(2,1)S(1)}, bf16[1024,200]{0,1:T(8,128)(2,1)}, u32[]{:S(2)}) copy-start(bf16[1024,200]{0,1:T(8,128)(2,1)} %param.13) | copy-start | bytes 1228804
  7.2 14.4 %copy-start.5 = (s32[200]{0:T(256)S(1)}, s32[200]{0:T(256)}, u32[]{:S(2)}) copy-start(s32[200]{0:T(256)} %param.17) | copy-start | bytes 2404
  7.2 14.6 %copy-start.7 = (s32[96]{0:T(128)S(1)}, s32[96]{0:T(128)}, u32[]{:S(2)}) copy-start(s32[96]{0:T(128)} %param.16) | copy-start | bytes 1156
  7.2 245.0 %all-reduce.3.cloned.1.call-start = ((), (), s32[]{:S(2)}) async-start(), calls=%async_computation | async-start | bytes 983040
  10.2 19.6 %collective-permute-start = (bf16[1024,320]{0,1:T(8,128)(2,1)S(1)}, bf16[1024,320]{0,1:T(8,128)(2,1)}, u32[]{:S(2)}, u32[]{:S(2)}) collective-permute-start(bf16[1024,320]{0,1:T(8,128)(2,1)S(1)} %bitcast.30), channel_id=1, source_target_pairs={{0,2},{1,3},{2,4},{3,5},{4,6},{5,7},{6,8},{7,9},{8,10},{9,11},{10,... | collective-permute-start | bytes 1966088 | tf_op jit(solution)/shard_map/ppermute | solution.py:17
  13.6 22.1 %collective-permute-start.1 = (bf16[1024,320]{0,1:T(8,128)(2,1)S(1)}, bf16[1024,320]{0,1:T(8,128)(2,1)}, u32[]{:S(2)}, u32[]{:S(2)}) collective-permute-start(bf16[1024,320]{0,1:T(8,128)(2,1)S(1)} %bitcast.31), channel_id=1, source_target_pairs={{0,1},{1,2},{2,3},{3,4},{4,5},{5,6},{6,7},{7,8},{8,9},{9,10},{10,1... | collective-permute-start | bytes 1966088 | tf_op jit(solution)/shard_map/ppermute | solution.py:17
  15.5 21.3 %collective-permute-start.2 = (bf16[1024,320]{0,1:T(8,128)(2,1)S(1)}, bf16[1024,320]{0,1:T(8,128)(2,1)}, u32[]{:S(2)}, u32[]{:S(2)}) collective-permute-start(bf16[1024,320]{0,1:T(8,128)(2,1)S(1)} %bitcast.32), channel_id=1, source_target_pairs={{1,0},{2,1},{3,2},{4,3},{5,4},{6,5},{7,6},{8,7},{9,8},{10,9},{11,1... | collective-permute-start | bytes 1966088 | tf_op jit(solution)/shard_map/ppermute | solution.py:17
  19.2 23.9 %collective-permute-start.3 = (bf16[1024,320]{0,1:T(8,128)(2,1)S(1)}, bf16[1024,320]{0,1:T(8,128)(2,1)}, u32[]{:S(2)}, u32[]{:S(2)}) collective-permute-start(bf16[1024,320]{0,1:T(8,128)(2,1)S(1)} %bitcast.33), channel_id=1, source_target_pairs={{2,0},{3,1},{4,2},{5,3},{6,4},{7,5},{8,6},{9,7},{10,8},{11,9},{12,... | collective-permute-start | bytes 1966088 | tf_op jit(solution)/shard_map/ppermute | solution.py:17
  22.7 23.2 %copy-start.4 = (s32[96,3]{0,1:T(4,128)S(1)}, s32[96,3]{0,1:T(4,128)}, u32[]{:S(2)}) copy-start(s32[96,3]{0,1:T(4,128)} %param.15) | copy-start | bytes 3460
  44.2 1.7 copy-start.2
  45.9 10.6 %copy-start.8 = (u32[256]{0:T(256)S(1)}, u32[256]{0:T(256)}, u32[]{:S(2)}) copy-start(u32[256]{0:T(256)} %constant.60) | copy-start | bytes 3076
  55.1 217.3 %copy-start.6 = (f32[5]{0:T(128)S(1)}, f32[5]{0:T(128)}, u32[]{:S(2)}) copy-start(f32[5]{0:T(128)} %constant.57) | copy-start | bytes 64
  253.1 20.6 %copy-start.3 = (f32[5,5,64]{2,1,0:T(8,128)}, f32[5,5,64]{2,1,0:T(8,128)S(1)}, u32[]{:S(2)}) copy-start(f32[5,5,64]{2,1,0:T(8,128)S(1)} %reshape.60) | copy-start | bytes 19204
Sparse Core Ops, SparseCore 0:
  56.6 195.5 all-reduce.2
where the time goes:
time: 281 us; the launch traced here: 280 us
  waiting for transfers between devices  211 us (75%)
  blocking collectives  15 us (5%)
  between operations  14.9 us (5%)
  local copies, waits for them, and re-layouts  11.7 us (4%)
  starting transfers between devices  10.9 us (4%)
  other arithmetic  6.12 us (2%)
  matrix products  6.11 us (2%)
  loops' own time  4.32 us (2%)
    unnamed x2, waiting for transfers between devices  195 us
    ppermute x4, waiting for transfers between devices, passed_along(): lax.ppermute(value, axis, [(source, source + steps) for source in range(i...  16.9 us
    all_gather x1, blocking collectives, local(): all_scenarios = lax.all_gather(profit, 'scen', axis=2, tiled=True)  15 us
    ppermute x4, starting transfers between devices, passed_along(): lax.ppermute(value, axis, [(source, source + steps) for source in range(i...  10.9 us
    unnamed x25, local copies, waits for them, and re-layouts  7.81 us
  transfers between devices with their start and end apart: 5, of which 4 were waited for; matrix products, arithmetic and copies ran while one was open for 2% of the time, Pallas kernels for 0%

commit v1 on v0

v1 whole, which is shorter than its diff:
```python
import jax
import jax.numpy as jnp
from jax import lax
from jax.experimental import pallas as pl
from jax.experimental.pallas import tpu as pltpu
from jax.sharding import PartitionSpec as P

BLK = 1024
HORIZONS = 5
CAP = 2
DESK_DEV = 5
ROWS = 8
LANES = 256
TAIL = 7

horizon_weights = (1.0, 1.0, 2.0, 2.0, 6.0)


def swap_pairs(count):
    near, far, chip_near, chip_far = [], [], [], []
    for index in range(count):
        near.append((index, index ^ 1))
        other = ((index + 1) ^ 1) - 1
        if 0 <= other < count:
            far.append((index, other))
        chip, core = divmod(index, 2)
        chip_near.append((index, (chip ^ 1) * 2 + core))
        other = ((chip + 1) ^ 1) - 1
        if 0 <= other < count // 2:
            chip_far.append((index, other * 2 + core))
    return near, far, chip_near, chip_far


def shocks_kernel(loadings_t, reduced_t, shocks):
    shocks[...] = lax.dot_general(
        reduced_t[...], loadings_t[...], (((1,), (0,)), ((), ())), preferred_element_type=jnp.float32
    ).astype(jnp.bfloat16)


def lane_row(tile):
    return jnp.concatenate([tile[q : q + 1, :] for q in range(tile.shape[0])], axis=1)


def masked_rows(shocks, bucket_tile):
    bucket = jnp.broadcast_to(lane_row(bucket_tile), shocks.shape)
    value = shocks.astype(jnp.float32)
    pieces = [jnp.where(bucket >= h, value, 0.0) for h in range(HORIZONS)]
    return jnp.concatenate(pieces, axis=0).astype(jnp.bfloat16)


def packed_tail(tail):
    count = tail.shape[0]
    row = lax.broadcasted_iota(jnp.int32, (count, 64), 0) % ROWS
    pieces = []
    for q in range(4):
        piece = jnp.where(row == DESK_DEV, pltpu.roll(tail, DESK_DEV - q, 0), 0.0)
        if q == 0:
            piece = jnp.where(row == DESK_DEV + 1, pltpu.roll(tail, DESK_DEV - 3, 0), piece)
        pieces.append(piece)
    return jnp.concatenate(pieces, axis=1)


def delta_kernel(own, buckets, sens_t, owner_row_ref, out):
    desks = sens_t.shape[0]
    fac_count = out.shape[0]
    count = fac_count * ROWS
    device = lax.axis_index("fac")
    owner_row = owner_row_ref[...]
    groups = lax.broadcasted_iota(jnp.int32, (fac_count, desks), 0)
    member = jnp.where(groups == jnp.broadcast_to(owner_row, (fac_count, desks)), 1.0, 0.0)
    before = jnp.where(
        lax.broadcasted_iota(jnp.int32, (desks, desks), 0)
        < lax.broadcasted_iota(jnp.int32, (desks, desks), 1),
        1.0,
        0.0,
    )
    prefix = lax.dot_general(
        member.astype(jnp.bfloat16), before.astype(jnp.bfloat16), (((1,), (0,)), ((), ())),
        preferred_element_type=jnp.float32,
    )
    rank = jnp.sum(prefix * member, axis=0, keepdims=True).astype(jnp.int32)
    slot_row = owner_row * ROWS + rank
    placement = jnp.where(
        lax.broadcasted_iota(jnp.int32, (count, desks), 0)
        == jnp.broadcast_to(slot_row, (count, desks)),
        1.0,
        0.0,
    ).astype(jnp.bfloat16)
    placed = lax.dot_general(
        placement, sens_t[...], (((1,), (0,)), ((), ())), preferred_element_type=jnp.float32
    ).astype(jnp.bfloat16)
    masked = masked_rows(own[...], buckets[device])
    delta = lax.dot_general(
        placed, masked, (((1,), (1,)), ((), ())), preferred_element_type=jnp.float32
    )
    packed = delta[:, :LANES] + packed_tail(delta[:, LANES:])
    out[...] = packed.reshape(fac_count, ROWS, LANES)


def gamma_kernel(
    block_owner, block_list, desk_owner, own, near, far, chip_near, chip_far, buckets,
    owner_row_ref, gamma, delta, out,
):
    blocks = block_owner.shape[0]
    desks = desk_owner.shape[0]
    device = lax.axis_index("fac")
    live = jnp.int32(0)
    first = jnp.int32(0)
    second = jnp.int32(0)
    for block in reversed(range(blocks)):
        hit = block_owner[block] == device
        second = jnp.where(hit, first, second)
        first = jnp.where(hit, block, first)
        live = live + jnp.where(hit, 1, 0)
    core = device % 2
    chip = (device // 2) % 2
    out[...] = delta[...]
    width = HORIZONS * own.shape[0]

    def pick(block):
        offset = block - device
        towards = jnp.where(core == 0, offset, -offset)
        chip_towards = jnp.where(chip == 0, offset, -offset)
        code = jnp.where(
            offset == 0,
            0,
            jnp.where(
                jnp.abs(offset) == 1,
                jnp.where(towards > 0, 1, 2),
                jnp.where(chip_towards > 0, 3, 4),
            ),
        )
        value = own[...]
        for index, ref in ((1, near), (2, far), (3, chip_near), (4, chip_far)):
            value = jnp.where(code == index, ref[...], value)
        return masked_rows(value, buckets[block])

    for slot, block_index in enumerate((first, second)):
        @pl.when(slot < live)
        def _(slot=slot, block_index=block_index):
            row_part = pick(block_list[0, block_index])
            col_part = pick(block_list[1, block_index])
            desk = block_list[2, block_index]
            product = lax.dot_general(
                row_part, gamma[slot], (((1,), (0,)), ((), ())), preferred_element_type=jnp.float32
            )
            quad = 0.5 * jnp.sum(col_part.astype(jnp.float32) * product, axis=1, keepdims=True)
            diagonal = lax.broadcasted_iota(jnp.int32, (width, width), 0) == lax.broadcasted_iota(
                jnp.int32, (width, width), 1
            )
            quad_row = jnp.sum(
                jnp.where(diagonal, jnp.broadcast_to(quad, (width, width)), 0.0),
                axis=0,
                keepdims=True,
            )
            owner = desk_owner[desk]
            owner_row = owner_row_ref[...]
            earlier = jnp.logical_and(
                owner_row == owner, lax.broadcasted_iota(jnp.int32, (1, desks), 1) < desk
            )
            rank = jnp.sum(jnp.where(earlier, 1.0, 0.0)).astype(jnp.int32)
            tail = quad_row[:, LANES:]
            tail_row = jnp.concatenate([tail] * 4, axis=1)
            quarter = lax.broadcasted_iota(jnp.int32, (ROWS, LANES), 1) // 64
            row = lax.broadcasted_iota(jnp.int32, (ROWS, LANES), 0)
            addend = jnp.where(
                row == rank, jnp.broadcast_to(quad_row[:, :LANES], (ROWS, LANES)), 0.0
            )
            addend = addend + jnp.where(
                jnp.logical_and(row == DESK_DEV + rank // 4, quarter == rank % 4),
                jnp.broadcast_to(tail_row, (ROWS, LANES)),
                0.0,
            )
            out[owner] = out[owner] + addend


def sum_kernel(received, packed, profit):
    total = jnp.sum(received[...], axis=0)
    packed[...] = total
    for h in range(HORIZONS - 1):
        for j in range(DESK_DEV):
            profit[j, h : h + 1, :] = total[j : j + 1, 64 * h : 64 * h + 64]
    for j in range(DESK_DEV):
        row = DESK_DEV + j // 4
        profit[j, HORIZONS - 1 : HORIZONS, :] = total[row : row + 1, 64 * (j % 4) : 64 * (j % 4) + 64]


def tail_kernel(own, other1, other2, other3, shortfall, adjusted):
    parts = 4
    lanes = 128
    joined = -jnp.concatenate([own[...], other1[...], other2[...], other3[...]], axis=0)
    joined = jnp.concatenate([joined, jnp.zeros((lanes - parts * ROWS, LANES), jnp.float32)], axis=0)
    columns = jnp.transpose(joined)
    values = columns.reshape(4, 8, 8, lanes)
    lowest = -jnp.inf

    def across(value, op, axes):
        return op(value, axis=axes, keepdims=True)

    def over_parts(value, op):
        value = op(value, pltpu.roll(value, lanes - ROWS, 3))
        return op(value, pltpu.roll(value, lanes - 2 * ROWS, 3))

    lane = lax.broadcasted_iota(jnp.int32, (4, 1, 1, lanes), 3)

    def spread(value):
        value = jnp.where(lane < ROWS, value, 0.0)
        value = value + pltpu.roll(value, ROWS, 3)
        return value + pltpu.roll(value, 2 * ROWS, 3)

    total = jnp.zeros((4, 1, 1, lanes), jnp.float32)
    left = jnp.full((4, 1, 1, lanes), float(TAIL), jnp.float32)
    for _ in range(TAIL):
        best = jnp.max(jnp.max(values, axis=1, keepdims=True), axis=2, keepdims=True)
        best = spread(over_parts(best, jnp.maximum))
        same = values == jnp.broadcast_to(best, values.shape)
        count = jnp.sum(
            jnp.sum(jnp.where(same, 1.0, 0.0), axis=1, keepdims=True), axis=2, keepdims=True
        )
        count = over_parts(count, jnp.add)
        taken = jnp.minimum(count, left)
        total = total + jnp.where(taken > 0.0, taken * best, 0.0)
        left = left - taken
        values = jnp.where(same, lowest, values)
    mean = (total * (1.0 / TAIL)).reshape(4, lanes)
    square = jnp.concatenate([mean, jnp.zeros((lanes - 4, lanes), jnp.float32)], axis=0)
    flipped = jnp.transpose(square)[:ROWS, :]
    top = square[:ROWS, :]
    fifth = pltpu.roll(top, lanes - 1, 1)
    last = pltpu.roll(pltpu.roll(top, lanes - 2, 1), 4, 0)
    row = lax.broadcasted_iota(jnp.int32, (ROWS, lanes), 0)
    col = lax.broadcasted_iota(jnp.int32, (ROWS, lanes), 1)
    result = jnp.where(col < 4, flipped, jnp.where(row == 4, last, fifth))
    shortfall[...] = result[:DESK_DEV, :HORIZONS]
    weight = jnp.zeros((ROWS, lanes), jnp.float32)
    for h, value in enumerate(horizon_weights):
        weight = jnp.where(col == h, value, weight)
    used = jnp.where(jnp.logical_and(col < HORIZONS, row < DESK_DEV), result, 0.0)
    spent = jnp.sum(weight * used * used, axis=1, keepdims=True)
    diagonal = jnp.where(row == col, jnp.broadcast_to(spent, (ROWS, lanes)), 0.0)
    adjusted[...] = jnp.sqrt(jnp.sum(diagonal, axis=0, keepdims=True) + 1e-06)[:, :DESK_DEV]


VMEM = pl.BlockSpec(memory_space=pltpu.VMEM)
SMEM = pl.BlockSpec(memory_space=pltpu.SMEM)


def local(
    loadings, reduced_shocks, sensitivity, cross_gamma, block_list, block_owner, desk_owner, buckets
):
    fac_count = lax.axis_size("fac")
    scen_count = lax.axis_size("scen")
    s_dev = reduced_shocks.shape[1]
    f32 = jnp.float32
    shocks = pl.pallas_call(
        shocks_kernel,
        out_shape=jax.ShapeDtypeStruct((s_dev, BLK), jnp.bfloat16),
        in_specs=[VMEM, VMEM],
        out_specs=VMEM,
        name="shocks",
    )(loadings.T, reduced_shocks.T)
    moved = [lax.ppermute(shocks, "fac", pairs) for pairs in swap_pairs(fac_count)]
    tiles = buckets.reshape(fac_count, 8, 128)
    owner_row = desk_owner.reshape(1, -1)
    packed_shape = jax.ShapeDtypeStruct((fac_count, ROWS, LANES), f32)
    delta = pl.pallas_call(
        delta_kernel,
        out_shape=packed_shape,
        in_specs=[VMEM] * 4,
        out_specs=VMEM,
        name="delta",
    )(shocks, tiles, sensitivity.T, owner_row)
    terms = pl.pallas_call(
        gamma_kernel,
        out_shape=packed_shape,
        in_specs=[SMEM] * 3 + [VMEM] * 9,
        out_specs=VMEM,
        name="gamma",
    )(block_owner, block_list.T, desk_owner, shocks, *moved, tiles, owner_row, cross_gamma, delta)
    received = lax.all_to_all(terms, "fac", 0, 0, tiled=False)
    packed, profit = pl.pallas_call(
        sum_kernel,
        out_shape=(
            jax.ShapeDtypeStruct((ROWS, LANES), f32),
            jax.ShapeDtypeStruct((DESK_DEV, HORIZONS, s_dev), f32),
        ),
        in_specs=[VMEM],
        out_specs=(VMEM, VMEM),
        name="total",
    )(received)
    others = [
        lax.ppermute(packed, "scen", [(i, i ^ step) for i in range(scen_count)])
        for step in range(1, scen_count)
    ]
    shortfall, adjusted = pl.pallas_call(
        tail_kernel,
        out_shape=(
            jax.ShapeDtypeStruct((DESK_DEV, HORIZONS), f32),
            jax.ShapeDtypeStruct((1, DESK_DEV), f32),
        ),
        in_specs=[VMEM] * scen_count,
        out_specs=(VMEM, VMEM),
        name="tail",
    )(packed, *others)
    return (profit, shortfall, adjusted.reshape(DESK_DEV))


def solution(mesh):
    return jax.shard_map(
        local,
        mesh=mesh,
        in_specs=(
            P("fac", None),
            P(None, "scen"),
            P("fac", None),
            P("fac", None, None),
            P(),
            P(),
            P(),
            P(),
        ),
        out_specs=(P("fac", None, "scen"), P("fac", None), P("fac")),
        check_vma=False,
    )
```

time: 281 us -> 66.6 us (0.24)
  waiting for transfers between devices: 211 us -> 4.29 us
  Pallas kernels: 0 us -> 17.1 us
  between operations: 14.9 us -> 0.71 us
  blocking collectives: 15 us -> 29.1 us
  local copies, waits for them, and re-layouts: 11.7 us -> 1.96 us
  other arithmetic: 6.12 us -> 0 us
  matrix products: 6.11 us -> 0 us
  loops' own time: 4.32 us -> 0 us
    unnamed x2 -> x0, waiting for transfers between devices: 195 us -> none
    all_to_all x0 -> x1, blocking collectives: none -> 29.1 us  [local(): received = lax.all_to_all(terms, 'fac', 0, 0, tiled=False)]
    pallas_call x0 -> x5, Pallas kernels: none -> 17.1 us  [the longest x1 5.69 us: local(): pl.pallas_call(gamma_kernel, out_shape=packed_shape, in_specs=[SMEM] * 3...]
    all_gather x1 -> x0, blocking collectives: 15 us -> none  [local(): all_scenarios = lax.all_gather(profit, 'scen', axis=2, tiled=True)]
    ppermute x4 -> x7, waiting for transfers between devices: 16.9 us -> 4.29 us  [the longest x3 4.28 us: local(): lax.ppermute(packed, 'scen', [(i, i ^ step) for i in range(scen_count)])]
    dot_general x4 -> x0, matrix products: 6.11 us -> none  [the longest x1 2.9 us: add_block(): product = jnp.dot(matrix, col_part, preferred_element_type=jnp.float32)]
    unnamed x25 -> x14, local copies, waits for them, and re-layouts: 7.81 us -> 1.96 us
    another operation x1 -> x0, loops' own time: 4.32 us -> none  [local(): partial_value = lax.fori_loop(0, live_blocks, add_block, partial_value)]
  transfers between devices with their start and end apart: 5 -> 7, of which waited for: 4 -> 2; matrix products, arithmetic and copies ran while one was open for 2% -> 0% of each run, Pallas kernels for 0% -> 5%
where the time goes in v1:
time: 66.6 us; the launch traced here: 65.8 us
  blocking collectives  29.1 us (44%)
  Pallas kernels  17.1 us (26%)
  starting transfers between devices  12.7 us (19%)
  waiting for transfers between devices  4.29 us (6%)
  local copies, waits for them, and re-layouts  1.96 us (3%)
  between operations  0.71 us (1%)
    all_to_all x1, blocking collectives, local(): received = lax.all_to_all(terms, 'fac', 0, 0, tiled=False)  29.1 us
    ppermute x4, starting transfers between devices, local(): lax.ppermute(shocks, 'fac', pairs)  8.59 us
    pallas_call x1, Pallas kernels, local(): pl.pallas_call(gamma_kernel, out_shape=packed_shape, in_specs=[SMEM] * 3...  5.69 us
    ppermute x3, waiting for transfers between devices, local(): lax.ppermute(packed, 'scen', [(i, i ^ step) for i in range(scen_count)])  4.28 us
    ppermute x3, starting transfers between devices, local(): lax.ppermute(packed, 'scen', [(i, i ^ step) for i in range(scen_count)])  4.09 us
    pallas_call x1, Pallas kernels, local(): pl.pallas_call(tail_kernel, out_shape=(jax.ShapeDtypeStruct((DESK_DEV, HO...  3.72 us
    pallas_call x1, Pallas kernels, local(): pl.pallas_call(delta_kernel, out_shape=packed_shape, in_specs=[VMEM] * 4,...  3.17 us
    pallas_call x1, Pallas kernels, local(): pl.pallas_call(shocks_kernel, out_shape=jax.ShapeDtypeStruct((s_dev, BLK)...  2.7 us
  transfers between devices with their start and end apart: 7, of which 2 were waited for; matrix products, arithmetic and copies ran while one was open for 0% of the time, Pallas kernels for 5%

profile of v1, /device:TPU:2, one launch (start us, length us, event | category | flops | bytes accessed | tf_op | source)
XLA Modules:
  0.0 65.8 jit_solution(18010620157691230829)
XLA Ops:
  0.6 2.7 %shocks.1.own = bf16[64,1024]{1,0:T(8,128)(2,1)} custom-call(bf16[1000,1024]{1,0:T(8,128)(2,1)} %bitcast.7, bf16[64,1000]{1,0:T(8,128)(2,1)} %bitcast.11), custom_call_target="tpu_custom_call" | custom-call | tf_op jit(solution)/shard_map/shocks/pallas_call | solution.py:255
  3.3 3.4 %collective-permute-start.3 = (bf16[64,1024]{1,0:T(8,128)(2,1)}, bf16[64,1024]{1,0:T(8,128)(2,1)S(1)}, u32[]{:S(2)}, u32[]{:S(2)}) collective-permute-start(bf16[64,1024]{1,0:T(8,128)(2,1)} %shocks.1.own), channel_id=1, source_target_pairs={{2,4},{3,5},{4,2},{5,3},{6,8},{7,9},{8,6},{9,7},{10,12},{11,13},{1... | collective-permute-start | bytes 393224 | tf_op jit(solution)/shard_map/ppermute | solution.py:262
  6.7 0.1 collective-permute-start.2
  6.8 2.8 %collective-permute-start.1 = (bf16[64,1024]{1,0:T(8,128)(2,1)}, bf16[64,1024]{1,0:T(8,128)(2,1)S(1)}, u32[]{:S(2)}, u32[]{:S(2)}) collective-permute-start(bf16[64,1024]{1,0:T(8,128)(2,1)} %shocks.1.own), channel_id=1, source_target_pairs={{1,2},{2,1},{3,4},{4,3},{5,6},{6,5},{7,8},{8,7},{9,10},{10,9},{11,... | collective-permute-start | bytes 393224 | tf_op jit(solution)/shard_map/ppermute | solution.py:262
  9.6 2.3 %collective-permute-start = (bf16[64,1024]{1,0:T(8,128)(2,1)}, bf16[64,1024]{1,0:T(8,128)(2,1)S(1)}, u32[]{:S(2)}, u32[]{:S(2)}) collective-permute-start(bf16[64,1024]{1,0:T(8,128)(2,1)} %shocks.1.own), channel_id=1, source_target_pairs={{0,1},{1,0},{2,3},{3,2},{4,5},{5,4},{6,7},{7,6},{8,9},{9,8},{10,11... | collective-permute-start | bytes 393224 | tf_op jit(solution)/shard_map/ppermute | solution.py:262
  11.9 3.2 %delta.1 = f32[64,8,256]{2,1,0:T(8,128)} custom-call(bf16[64,1024]{1,0:T(8,128)(2,1)} %shocks.1.own, s32[64,8,128]{2,1,0:T(8,128)} %bitcast.8, bf16[200,1024]{1,0:T(8,128)(2,1)} %bitcast.10, s32[1,200]{1,0:T(1,128)} %bitcast.12), custom_call_target="tpu_custom_call" | custom-call | tf_op jit(solution)/shard_map/delta/pallas_call | solution.py:266
  15.1 0.0 collective-permute-done.3.chip_far
  15.1 0.0 copy-start
  15.1 0.0 collective-permute-done.2.chip_near
  15.1 0.0 copy-start.1
  15.1 0.0 collective-permute-done.1.far
  15.2 0.0 copy-start.2
  15.2 0.0 collective-permute-done.near
  15.2 0.0 copy-start.3
  15.2 0.6 copy-done
  15.8 0.1 copy-done.1
  15.8 0.0 copy-done.2
  15.9 0.1 copy-done.3
  15.9 5.7 %gamma.2 = f32[64,8,256]{2,1,0:T(8,128)} custom-call(s32[96]{0:T(128)} %block_owner.1, s32[3,96]{1,0:T(4,128)} %bitcast.14, s32[200]{0:T(256)} %desk_owner.1, bf16[64,1024]{1,0:T(8,128)(2,1)} %shocks.1.own, bf16[64,1024]{1,0:T(8,128)(2,1)} %copy-done.3, bf16[64,1024]{1,0:T(8,128)(2,1)} %copy-done.2, bf16[64,1024]{1,0:T(8,128)(2,1)} %copy-done.1, ...), custom_call_target="tpu_custom_call" | custom-call | tf_op jit(solution)/shard_map/gamma/pallas_call | solution.py:273
  21.6 29.1 %all_to_all.5.received = f32[64,8,256]{2,1,0:T(8,128)} all-to-all(f32[64,8,256]{2,1,0:T(8,128)} %gamma.2), channel_id=1, replica_groups=mesh['scen'=4,'fac'=64] {'fac'}, dimensions={0} | all-to-all | bytes 1048576 | tf_op jit(solution)/shard_map/all_to_all | solution.py:280
  50.7 1.8 %total.1 = (f32[8,256]{1,0:T(8,128)}, f32[5,5,64]{2,1,0:T(8,128)}) custom-call(f32[64,8,256]{2,1,0:T(8,128)} %all_to_all.5.received), custom_call_target="tpu_custom_call" | custom-call | tf_op jit(solution)/shard_map/total/pallas_call | solution.py:281
  52.5 3.0 %collective-permute-start.6 = (f32[8,256]{1,0:T(8,128)}, f32[8,256]{1,0:T(8,128)S(1)}, u32[]{:S(2)}, u32[]{:S(2)}) collective-permute-start(f32[8,256]{1,0:T(8,128)} %get-tuple-element.8.own), channel_id=1, source_target_pairs={{0,192},{64,128},{128,64},{192,0},{1,193},{65,129},{129,65},{193,1... | collective-permute-start | bytes 24584 | tf_op jit(solution)/shard_map/ppermute | solution.py:292
  55.5 0.6 collective-permute-start.5
  56.1 0.5 collective-permute-start.4
  56.6 1.0 %collective-permute-done.6.other3 = f32[8,256]{1,0:T(8,128)S(1)} collective-permute-done((f32[8,256]{1,0:T(8,128)}, f32[8,256]{1,0:T(8,128)S(1)}, u32[]{:S(2)}, u32[]{:S(2)}) %collective-permute-start.6) | collective-permute-done | bytes 8224 | tf_op jit(solution)/shard_map/ppermute | solution.py:292
  57.5 0.0 copy-start.4
  57.5 3.3 %collective-permute-done.5.other2 = f32[8,256]{1,0:T(8,128)S(1)} collective-permute-done((f32[8,256]{1,0:T(8,128)}, f32[8,256]{1,0:T(8,128)S(1)}, u32[]{:S(2)}, u32[]{:S(2)}) %collective-permute-start.5) | collective-permute-done | bytes 8224 | tf_op jit(solution)/shard_map/ppermute | solution.py:292
  60.9 0.0 copy-start.5
  60.9 0.0 collective-permute-done.4.other1
  60.9 0.0 copy-done.4
  60.9 0.6 copy-done.5
  61.5 0.0 copy-start.6
  61.5 0.6 copy-done.6
  62.1 3.7 %tail.1 = (f32[5,5]{1,0:T(8,128)}, f32[1,5]{1,0:T(1,128)}) custom-call(f32[8,256]{1,0:T(8,128)} %get-tuple-element.8.own, f32[8,256]{1,0:T(8,128)} %copy-done.6, f32[8,256]{1,0:T(8,128)} %copy-done.5, f32[8,256]{1,0:T(8,128)} %copy-done.4), custom_call_target="tpu_custom_call" | custom-call | tf_op jit(solution)/shard_map/tail/pallas_call | solution.py:295
Async XLA Ops:
  3.3 11.8 %collective-permute-start.3 = (bf16[64,1024]{1,0:T(8,128)(2,1)}, bf16[64,1024]{1,0:T(8,128)(2,1)S(1)}, u32[]{:S(2)}, u32[]{:S(2)}) collective-permute-start(bf16[64,1024]{1,0:T(8,128)(2,1)} %shocks.1.own), channel_id=1, source_target_pairs={{2,4},{3,5},{4,2},{5,3},{6,8},{7,9},{8,6},{9,7},{10,12},{11,13},{1... | collective-permute-start | bytes 393224 | tf_op jit(solution)/shard_map/ppermute | solution.py:262
  6.7 8.4 %collective-permute-start.2 = (bf16[64,1024]{1,0:T(8,128)(2,1)}, bf16[64,1024]{1,0:T(8,128)(2,1)S(1)}, u32[]{:S(2)}, u32[]{:S(2)}) collective-permute-start(bf16[64,1024]{1,0:T(8,128)(2,1)} %shocks.1.own), channel_id=1, source_target_pairs={{0,2},{1,3},{2,0},{3,1},{4,6},{5,7},{6,4},{7,5},{8,10},{9,11},{10,... | collective-permute-start | bytes 393224 | tf_op jit(solution)/shard_map/ppermute | solution.py:262
  6.8 8.3 %collective-permute-start.1 = (bf16[64,1024]{1,0:T(8,128)(2,1)}, bf16[64,1024]{1,0:T(8,128)(2,1)S(1)}, u32[]{:S(2)}, u32[]{:S(2)}) collective-permute-start(bf16[64,1024]{1,0:T(8,128)(2,1)} %shocks.1.own), channel_id=1, source_target_pairs={{1,2},{2,1},{3,4},{4,3},{5,6},{6,5},{7,8},{8,7},{9,10},{10,9},{11,... | collective-permute-start | bytes 393224 | tf_op jit(solution)/shard_map/ppermute | solution.py:262
  9.6 5.5 %collective-permute-start = (bf16[64,1024]{1,0:T(8,128)(2,1)}, bf16[64,1024]{1,0:T(8,128)(2,1)S(1)}, u32[]{:S(2)}, u32[]{:S(2)}) collective-permute-start(bf16[64,1024]{1,0:T(8,128)(2,1)} %shocks.1.own), channel_id=1, source_target_pairs={{0,1},{1,0},{2,3},{3,2},{4,5},{5,4},{6,7},{7,6},{8,9},{9,8},{10,11... | collective-permute-start | bytes 393224 | tf_op jit(solution)/shard_map/ppermute | solution.py:262
  15.1 0.6 copy-start
  15.1 0.7 %copy-start.1 = (bf16[64,1024]{1,0:T(8,128)(2,1)}, bf16[64,1024]{1,0:T(8,128)(2,1)S(1)}, u32[]{:S(2)}) copy-start(bf16[64,1024]{1,0:T(8,128)(2,1)S(1)} %collective-permute-done.2.chip_near) | copy-start | bytes 393220
  15.2 0.7 %copy-start.2 = (bf16[64,1024]{1,0:T(8,128)(2,1)}, bf16[64,1024]{1,0:T(8,128)(2,1)S(1)}, u32[]{:S(2)}) copy-start(bf16[64,1024]{1,0:T(8,128)(2,1)S(1)} %collective-permute-done.1.far) | copy-start | bytes 393220
  15.2 0.8 %copy-start.3 = (bf16[64,1024]{1,0:T(8,128)(2,1)}, bf16[64,1024]{1,0:T(8,128)(2,1)S(1)}, u32[]{:S(2)}) copy-start(bf16[64,1024]{1,0:T(8,128)(2,1)S(1)} %collective-permute-done.near) | copy-start | bytes 393220
  52.5 5.1 %collective-permute-start.6 = (f32[8,256]{1,0:T(8,128)}, f32[8,256]{1,0:T(8,128)S(1)}, u32[]{:S(2)}, u32[]{:S(2)}) collective-permute-start(f32[8,256]{1,0:T(8,128)} %get-tuple-element.8.own), channel_id=1, source_target_pairs={{0,192},{64,128},{128,64},{192,0},{1,193},{65,129},{129,65},{193,1... | collective-permute-start | bytes 24584 | tf_op jit(solution)/shard_map/ppermute | solution.py:292
  55.5 5.4 %collective-permute-start.5 = (f32[8,256]{1,0:T(8,128)}, f32[8,256]{1,0:T(8,128)S(1)}, u32[]{:S(2)}, u32[]{:S(2)}) collective-permute-start(f32[8,256]{1,0:T(8,128)} %get-tuple-element.8.own), channel_id=1, source_target_pairs={{0,128},{64,192},{128,0},{192,64},{1,129},{65,193},{129,1},{193,65... | collective-permute-start | bytes 24584 | tf_op jit(solution)/shard_map/ppermute | solution.py:292
  56.1 4.7 %collective-permute-start.4 = (f32[8,256]{1,0:T(8,128)}, f32[8,256]{1,0:T(8,128)S(1)}, u32[]{:S(2)}, u32[]{:S(2)}) collective-permute-start(f32[8,256]{1,0:T(8,128)} %get-tuple-element.8.own), channel_id=1, source_target_pairs={{0,64},{64,0},{128,192},{192,128},{1,65},{65,1},{129,193},{193,129... | collective-permute-start | bytes 24584 | tf_op jit(solution)/shard_map/ppermute | solution.py:292
  57.5 3.3 %copy-start.4 = (f32[8,256]{1,0:T(8,128)}, f32[8,256]{1,0:T(8,128)S(1)}, u32[]{:S(2)}) copy-start(f32[8,256]{1,0:T(8,128)S(1)} %collective-permute-done.6.other3) | copy-start | bytes 24580
  60.9 0.6 copy-start.5
  61.5 0.6 copy-start.6

commit v2 on v1

v2 whole, which is shorter than its diff:
```python
import jax
import jax.numpy as jnp
from jax import lax
from jax.experimental import pallas as pl
from jax.experimental.pallas import tpu as pltpu
from jax.sharding import PartitionSpec as P

BLK = 1024
HORIZONS = 5
CAP = 2
DESK_DEV = 5
ROWS = 8
LANES = 256
TAIL = 7
CHUNKS = 4

horizon_weights = (1.0, 1.0, 2.0, 2.0, 6.0)


def swap_pairs(count):
    near, far, chip_near, chip_far = [], [], [], []
    for index in range(count):
        near.append((index, index ^ 1))
        other = ((index + 1) ^ 1) - 1
        if 0 <= other < count:
            far.append((index, other))
        chip, core = divmod(index, 2)
        chip_near.append((index, (chip ^ 1) * 2 + core))
        other = ((chip + 1) ^ 1) - 1
        if 0 <= other < count // 2:
            chip_far.append((index, other * 2 + core))
    return near, far, chip_near, chip_far


def block_code(block, device):
    offset = block - device
    side = jnp.where(device % 2 == 0, offset, -offset)
    chip_side = jnp.where((device // 2) % 2 == 0, offset, -offset)
    beside = jnp.where(side > 0, 1, 2)
    apart = jnp.where(chip_side > 0, 3, 4)
    return jnp.where(offset == 0, 0, jnp.where(jnp.abs(offset) == 1, beside, apart))


def shocks_kernel(
    loadings_t, reduced_t, tiles_hbm, sens_hbm, owner_hbm, block_owner_hbm, block_list_hbm,
    desk_owner_hbm, shocks, tiles, sens_t, owner_row, meta, weights, factors, block_owner,
    block_list, desk_owner, sems,
):
    parts = CHUNKS
    span = BLK // parts
    copies = [pltpu.make_async_copy(reduced_t, factors, sems.at[parts])]
    for part in range(parts):
        window = pl.ds(part * span, span)
        copies.append(
            pltpu.make_async_copy(loadings_t.at[:, window], weights.at[:, window], sems.at[part])
        )
    scalars = [
        pltpu.make_async_copy(block_owner_hbm, block_owner, sems.at[parts + 1]),
        pltpu.make_async_copy(block_list_hbm, block_list, sems.at[parts + 2]),
        pltpu.make_async_copy(desk_owner_hbm, desk_owner, sems.at[parts + 3]),
    ]
    later = [
        pltpu.make_async_copy(owner_hbm, owner_row, sems.at[parts + 4]),
        pltpu.make_async_copy(tiles_hbm, tiles, sems.at[parts + 5]),
        pltpu.make_async_copy(sens_hbm, sens_t, sems.at[parts + 6]),
    ]
    for copy in scalars + copies + later:
        copy.start()
    for copy in scalars:
        copy.wait()
    device = lax.axis_index("fac")
    live = jnp.int32(0)
    first = jnp.int32(0)
    second = jnp.int32(0)
    for block in reversed(range(block_owner.shape[0])):
        hit = block_owner[block] == device
        second = jnp.where(hit, first, second)
        first = jnp.where(hit, block, first)
        live = live + jnp.where(hit, 1, 0)
    meta[0] = live
    for slot, block in enumerate((first, second)):
        row = block_list[0, block]
        col = block_list[1, block]
        desk = block_list[2, block]
        meta[1 + 6 * slot] = row
        meta[2 + 6 * slot] = block_code(row, device)
        meta[3 + 6 * slot] = col
        meta[4 + 6 * slot] = block_code(col, device)
        meta[5 + 6 * slot] = desk
        meta[6 + 6 * slot] = desk_owner[desk]
    copies[0].wait()
    for part in range(parts):
        copies[1 + part].wait()
        window = pl.ds(part * span, span)
        shocks[:, window] = lax.dot_general(
            factors[...], weights[:, window], (((1,), (0,)), ((), ())),
            preferred_element_type=jnp.float32,
        ).astype(jnp.bfloat16)
    for copy in later:
        copy.wait()


def lane_row(tile):
    return jnp.concatenate([tile[q : q + 1, :] for q in range(tile.shape[0])], axis=1)


def masked_rows(shocks, bucket_tile):
    bucket = jnp.broadcast_to(lane_row(bucket_tile), shocks.shape)
    value = shocks.astype(jnp.float32)
    pieces = [jnp.where(bucket >= h, value, 0.0) for h in range(HORIZONS)]
    return jnp.concatenate(pieces, axis=0).astype(jnp.bfloat16)


def packed_tail(tail):
    count = tail.shape[0]
    row = lax.broadcasted_iota(jnp.int32, (count, 64), 0) % ROWS
    pieces = []
    for q in range(4):
        piece = jnp.where(row == DESK_DEV, pltpu.roll(tail, DESK_DEV - q, 0), 0.0)
        if q == 0:
            piece = jnp.where(row == DESK_DEV + 1, pltpu.roll(tail, DESK_DEV - 3, 0), piece)
        pieces.append(piece)
    return jnp.concatenate(pieces, axis=1)


def encoded(chunks):
    largest = jnp.max(jnp.abs(chunks), axis=1, keepdims=True)
    exponent = jnp.ceil(jnp.log2(jnp.maximum(largest, 2.0**-100))) - 14.0
    shape = chunks.shape
    exponent = jnp.broadcast_to(exponent, shape)
    row = lax.broadcasted_iota(jnp.int32, shape, 1)
    value = jnp.where(row == ROWS - 1, exponent, jnp.round(chunks * jnp.exp2(-exponent)))
    value = jnp.concatenate([value[:, :, :128], value[:, :, 128:]], axis=1)
    return value.astype(jnp.int32).astype(jnp.int16)


def delta_kernel(own, buckets, sens_t, owner_row_ref, gamma_hbm, out, coded, gamma, sem):
    copy = pltpu.make_async_copy(gamma_hbm, gamma, sem)
    copy.start()
    desks = sens_t.shape[0]
    fac_count = out.shape[0]
    count = fac_count * ROWS
    device = lax.axis_index("fac")
    owner_row = owner_row_ref[...]
    groups = lax.broadcasted_iota(jnp.int32, (fac_count, desks), 0)
    member = jnp.where(groups == jnp.broadcast_to(owner_row, (fac_count, desks)), 1.0, 0.0)
    before = jnp.where(
        lax.broadcasted_iota(jnp.int32, (desks, desks), 0)
        < lax.broadcasted_iota(jnp.int32, (desks, desks), 1),
        1.0,
        0.0,
    )
    prefix = lax.dot_general(
        member.astype(jnp.bfloat16), before.astype(jnp.bfloat16), (((1,), (0,)), ((), ())),
        preferred_element_type=jnp.float32,
    )
    rank = jnp.sum(prefix * member, axis=0, keepdims=True).astype(jnp.int32)
    slot_row = owner_row * ROWS + rank
    placement = jnp.where(
        lax.broadcasted_iota(jnp.int32, (count, desks), 0)
        == jnp.broadcast_to(slot_row, (count, desks)),
        1.0,
        0.0,
    ).astype(jnp.bfloat16)
    placed = lax.dot_general(
        placement, sens_t[...], (((1,), (0,)), ((), ())), preferred_element_type=jnp.float32
    ).astype(jnp.bfloat16)
    masked = masked_rows(own[...], buckets[device])
    delta = lax.dot_general(
        placed, masked, (((1,), (1,)), ((), ())), preferred_element_type=jnp.float32
    )
    packed = delta[:, :LANES] + packed_tail(delta[:, LANES:])
    chunks = packed.reshape(fac_count, ROWS, LANES)
    out[...] = chunks
    coded[...] = encoded(chunks)
    copy.wait()


def gamma_kernel(
    meta, own, near, far, chip_near, chip_far, buckets, owner_row_ref, gamma, delta, coded, out, sums,
):
    del coded
    desks = owner_row_ref.shape[1]
    width = HORIZONS * own.shape[0]
    live = meta[0]
    sums[...] = jnp.zeros(sums.shape, jnp.float32)

    def pick(block, code):
        value = own[...]
        for index, ref in ((1, near), (2, far), (3, chip_near), (4, chip_far)):
            value = jnp.where(code == index, ref[...], value)
        return masked_rows(value, buckets[block])

    for slot in range(CAP):
        @pl.when(slot < live)
        def _(slot=slot):
            row_part = pick(meta[1 + 6 * slot], meta[2 + 6 * slot])
            col_part = pick(meta[3 + 6 * slot], meta[4 + 6 * slot])
            desk = meta[5 + 6 * slot]
            owner = meta[6 + 6 * slot]
            product = lax.dot_general(
                row_part, gamma[slot], (((1,), (0,)), ((), ())), preferred_element_type=jnp.float32
            )
            quad = 0.5 * jnp.sum(col_part.astype(jnp.float32) * product, axis=1, keepdims=True)
            diagonal = lax.broadcasted_iota(jnp.int32, (width, width), 0) == lax.broadcasted_iota(
                jnp.int32, (width, width), 1
            )
            quad_row = jnp.sum(
                jnp.where(diagonal, jnp.broadcast_to(quad, (width, width)), 0.0),
                axis=0,
                keepdims=True,
            )
            earlier = jnp.logical_and(
                owner_row_ref[...] == owner, lax.broadcasted_iota(jnp.int32, (1, desks), 1) < desk
            )
            rank = jnp.sum(jnp.where(earlier, 1.0, 0.0), axis=1, keepdims=True).astype(jnp.int32)
            rank = jnp.broadcast_to(rank, (ROWS, LANES))
            tail_row = jnp.concatenate([quad_row[:, LANES:]] * 4, axis=1)
            quarter = lax.broadcasted_iota(jnp.int32, (ROWS, LANES), 1) // 64
            row = lax.broadcasted_iota(jnp.int32, (ROWS, LANES), 0)
            moved = jnp.where(rank >= 4, 4, 0)
            in_tail = jnp.logical_and(
                row == DESK_DEV + jnp.where(rank >= 4, 1, 0), quarter == rank - moved
            )
            sums[slot] = jnp.where(
                row == rank,
                jnp.broadcast_to(quad_row[:, :LANES], (ROWS, LANES)),
                jnp.where(in_tail, jnp.broadcast_to(tail_row, (ROWS, LANES)), 0.0),
            )

    first = meta[6]
    second = jnp.where(live > 1, meta[12], first)
    joint = jnp.where(first == second, 1.0, 0.0)

    @pl.when(live > 0)
    def _():
        one = delta[first] + sums[0] + joint * sums[1]
        out[first] = encoded(one[None])[0]

    @pl.when(live > 1)
    def _():
        two = delta[second] + sums[1] + joint * sums[0]
        out[second] = encoded(two[None])[0]


def sum_kernel(received, packed, profit):
    lanes = 128
    value = received[...].astype(jnp.int32).astype(jnp.float32)
    value = value.reshape(received.shape[0] * 2, ROWS, lanes)
    scale = jnp.exp2(value[:, ROWS - 1 :, :])
    total = value * jnp.broadcast_to(scale, value.shape)
    total = jnp.sum(total.reshape(received.shape[0], 2, ROWS, lanes), axis=0)
    low, high = total[0], total[1]
    low_turned = pltpu.roll(low, 64, 1)
    high_turned = pltpu.roll(high, 64, 1)
    row = lax.broadcasted_iota(jnp.int32, (ROWS, lanes), 0)
    fifth = pltpu.roll(low, ROWS - DESK_DEV, 0)
    for j, source, shift in (
        (1, low_turned, 4), (2, high, 3), (3, high_turned, 2), (4, low, 2),
    ):
        moved = pltpu.roll(source, ROWS - shift, 0)
        fifth = jnp.where(row == j, moved, fifth)
    for h, block in enumerate((low, low_turned, high, high_turned, fifth)):
        packed[ROWS * h : ROWS * h + ROWS, :] = block
        for j in range(DESK_DEV):
            profit[j, h : h + 1, :] = block[j : j + 1, :64]


def tail_kernel(own, other1, other2, other3, shortfall, adjusted):
    lanes = 128
    count = HORIZONS * ROWS
    lane = lax.broadcasted_iota(jnp.int32, (count, lanes), 1)
    filler = jnp.zeros((lanes - count, lanes), jnp.float32)
    columns = []
    for one, two in ((own, other1), (other2, other3)):
        pair = -jnp.where(lane < 64, one[...], pltpu.roll(two[...], 64, 1))
        columns.append(jnp.transpose(jnp.concatenate([pair, filler], axis=0)))
    values = jnp.concatenate(columns, axis=0).reshape(32, 8, lanes)
    total = jnp.zeros((1, lanes), jnp.float32)
    left = jnp.full((1, lanes), float(TAIL), jnp.float32)
    for _ in range(TAIL):
        best = jnp.max(jnp.max(values, axis=0), axis=0, keepdims=True)
        same = values == jnp.broadcast_to(best[None], values.shape)
        found = jnp.sum(jnp.sum(jnp.where(same, 1.0, 0.0), axis=0), axis=0, keepdims=True)
        taken = jnp.minimum(found, left)
        total = total + jnp.where(taken > 0.0, taken * best, 0.0)
        left = left - taken
        values = jnp.where(same, -jnp.inf, values)
    mean = jnp.broadcast_to(total * (1.0 / TAIL), (ROWS, lanes))
    row = lax.broadcasted_iota(jnp.int32, (ROWS, lanes), 0)
    by_horizon = mean
    weight = jnp.full((ROWS, lanes), horizon_weights[0], jnp.float32)
    for h in range(1, HORIZONS):
        by_horizon = jnp.where(row == h, pltpu.roll(mean, lanes - ROWS * h, 1), by_horizon)
        weight = jnp.where(row == h, horizon_weights[h], weight)
    weight = jnp.where(row < HORIZONS, weight, 0.0)
    spent = jnp.sum(weight * by_horizon * by_horizon, axis=0, keepdims=True)
    adjusted[...] = jnp.sqrt(spent + 1e-06)[:, :DESK_DEV]
    square = jnp.concatenate([by_horizon, jnp.zeros((lanes - ROWS, lanes), jnp.float32)], axis=0)
    shortfall[...] = jnp.transpose(square)[:DESK_DEV, :HORIZONS]


VMEM = pl.BlockSpec(memory_space=pltpu.VMEM)
SMEM = pl.BlockSpec(memory_space=pltpu.SMEM)
HBM = pl.BlockSpec(memory_space=pltpu.HBM)
ORDER = (0, 2, 1, 3)


def held(value):
    return pltpu.with_memory_space_constraint(value, pltpu.VMEM)


def resident(value):
    return pltpu.with_memory_space_constraint(value, pltpu.HBM)


def limited(mib):
    return pltpu.CompilerParams(vmem_limit_bytes=mib << 20)


def local(
    loadings, reduced_shocks, sensitivity, cross_gamma, block_list, block_owner, desk_owner, buckets
):
    fac_count = lax.axis_size("fac")
    scen_count = lax.axis_size("scen")
    factors, s_dev = reduced_shocks.shape
    desks = desk_owner.shape[0]
    f32 = jnp.float32
    bf16 = jnp.bfloat16
    i32 = jnp.int32
    tile_shape = (fac_count, 8, BLK // 8)
    shocks, tiles, sens_t, owner_row, meta = pl.pallas_call(
        shocks_kernel,
        out_shape=(
            pltpu.VMEM((s_dev, BLK), bf16),
            pltpu.VMEM(tile_shape, i32),
            pltpu.VMEM((desks, BLK), bf16),
            pltpu.VMEM((1, desks), i32),
            pltpu.SMEM((16,), i32),
        ),
        in_specs=[HBM] * 8,
        out_specs=(VMEM, VMEM, VMEM, VMEM, SMEM),
        scratch_shapes=[
            pltpu.VMEM((factors, BLK), bf16),
            pltpu.VMEM((s_dev, factors), bf16),
            pltpu.SMEM(block_owner.shape, i32),
            pltpu.SMEM(block_list.shape[::-1], i32),
            pltpu.SMEM(desk_owner.shape, i32),
            pltpu.SemaphoreType.DMA((CHUNKS + 7,)),
        ],
        name="shocks",
        compiler_params=limited(10),
    )(
        *map(
            resident,
            (
                loadings.T, reduced_shocks.T, buckets.reshape(tile_shape), sensitivity.T,
                desk_owner.reshape(1, desks), block_owner, block_list.T, desk_owner,
            ),
        )
    )
    pairs = swap_pairs(fac_count)
    moved = {index: held(lax.ppermute(shocks, "fac", pairs[index])) for index in ORDER}
    chunk_shape = (fac_count, ROWS, LANES)
    coded_shape = pltpu.VMEM((fac_count, 2 * ROWS, LANES // 2), jnp.int16)
    delta, coded, gamma = pl.pallas_call(
        delta_kernel,
        out_shape=(
            pltpu.VMEM(chunk_shape, f32), coded_shape, pltpu.VMEM(cross_gamma.shape, bf16)
        ),
        in_specs=[VMEM] * 4 + [HBM],
        out_specs=(VMEM, VMEM, VMEM),
        scratch_shapes=[pltpu.SemaphoreType.DMA],
        name="delta",
        compiler_params=limited(16),
    )(shocks, tiles, sens_t, owner_row, resident(cross_gamma))
    terms = pl.pallas_call(
        gamma_kernel,
        out_shape=coded_shape,
        in_specs=[SMEM] + [VMEM] * 10,
        out_specs=VMEM,
        scratch_shapes=[pltpu.VMEM((CAP, ROWS, LANES), f32)],
        input_output_aliases={10: 0},
        name="gamma",
        compiler_params=limited(16),
    )(meta, shocks, moved[0], moved[1], moved[2], moved[3], tiles, owner_row, gamma, delta, coded)
    received = held(lax.all_to_all(terms, "fac", 0, 0, tiled=False))
    packed, profit = pl.pallas_call(
        sum_kernel,
        out_shape=(
            pltpu.VMEM((HORIZONS * ROWS, 128), f32),
            jax.ShapeDtypeStruct((DESK_DEV, HORIZONS, s_dev), f32),
        ),
        in_specs=[VMEM],
        out_specs=(VMEM, VMEM),
        name="total",
        compiler_params=limited(8),
    )(received)
    others = [
        held(lax.ppermute(packed, "scen", [(i, i ^ step) for i in range(scen_count)]))
        for step in (1, 3, 2)
    ]
    shortfall, adjusted = pl.pallas_call(
        tail_kernel,
        out_shape=(
            jax.ShapeDtypeStruct((DESK_DEV, HORIZONS), f32),
            jax.ShapeDtypeStruct((1, DESK_DEV), f32),
        ),
        in_specs=[VMEM] * scen_count,
        out_specs=(VMEM, VMEM),
        name="tail",
        compiler_params=limited(8),
    )(packed, *others)
    return (profit, shortfall, adjusted.reshape(DESK_DEV))


def solution(mesh):
    return jax.shard_map(
        local,
        mesh=mesh,
        in_specs=(
            P("fac", None),
            P(None, "scen"),
            P("fac", None),
            P("fac", None, None),
            P(),
            P(),
            P(),
            P(),
        ),
        out_specs=(P("fac", None, "scen"), P("fac", None), P("fac")),
        check_vma=False,
    )
```

time: 66.6 us -> 53.3 us (0.80); the launches traced: 65.8 us -> 53.2 us
  Pallas kernels: 17.1 us -> 8.05 us
  blocking collectives: 29.1 us -> 26.1 us
  local copies, waits for them, and re-layouts: 1.96 us -> 0 us
  waiting for transfers between devices: 4.29 us -> 6.21 us
    pallas_call x4, Pallas kernels: 13.3 us -> 6.91 us  [the longest x1 2.72 us: local(): pl.pallas_call(delta_kernel, out_shape=(pltpu.VMEM(chunk_shape, f32), cod...]
    all_to_all x1, blocking collectives: 29.1 us -> 26.1 us  [local(): received = held(lax.all_to_all(terms, 'fac', 0, 0, tiled=False))]
    pallas_call x1, Pallas kernels: 3.72 us -> 1.14 us  [local(): pl.pallas_call(tail_kernel, out_shape=(jax.ShapeDtypeStruct((DESK_DEV, HO...]
    unnamed x14 -> x0, local copies, waits for them, and re-layouts: 1.96 us -> none
    ppermute x4, waiting for transfers between devices: 0.01 us -> 1.64 us  [local(): lax.ppermute(shocks, 'fac', pairs[index])]
    ppermute x4, starting transfers between devices: 8.59 us -> 7.58 us  [local(): lax.ppermute(shocks, 'fac', pairs[index])]
  transfers between devices with their start and end apart: 7 -> 7, of which waited for: 2 -> 3; matrix products, arithmetic and copies ran while one was open for 0% -> 0% of each run, Pallas kernels for 5% -> 5%
where the time goes in v2:
time: 53.3 us; the launch traced here: 53.2 us
  blocking collectives  26.1 us (49%)
  starting transfers between devices  12.1 us (23%)
  Pallas kernels  8.05 us (15%)
  waiting for transfers between devices  6.21 us (12%)
  between operations  0.72 us (1%)
    all_to_all x1, blocking collectives, local(): received = held(lax.all_to_all(terms, 'fac', 0, 0, tiled=False))  26.1 us
    ppermute x4, starting transfers between devices, local(): lax.ppermute(shocks, 'fac', pairs[index])  7.58 us
    ppermute x3, waiting for transfers between devices, local(): lax.ppermute(packed, 'scen', [(i, i ^ step) for i in range(scen_count)])  4.56 us
    ppermute x3, starting transfers between devices, local(): lax.ppermute(packed, 'scen', [(i, i ^ step) for i in range(scen_count)])  4.48 us
    pallas_call x1, Pallas kernels, local(): pl.pallas_call(delta_kernel, out_shape=(pltpu.VMEM(chunk_shape, f32), cod...  2.72 us
    pallas_call x1, Pallas kernels, local(): pl.pallas_call(shocks_kernel, out_shape=(pltpu.VMEM((s_dev, BLK), bf16),...  2.32 us
    ppermute x4, waiting for transfers between devices, local(): lax.ppermute(shocks, 'fac', pairs[index])  1.64 us
    pallas_call x1, Pallas kernels, local(): pl.pallas_call(tail_kernel, out_shape=(jax.ShapeDtypeStruct((DESK_DEV, HO...  1.14 us
  transfers between devices with their start and end apart: 7, of which 3 were waited for; matrix products, arithmetic and copies ran while one was open for 0% of the time, Pallas kernels for 5%

profile of v2, /device:TPU:2, one launch (start us, length us, event | category | flops | bytes accessed | tf_op | source)
XLA Modules:
  0.0 53.2 jit_solution(6137283035789479254)
XLA Ops:
  0.6 2.3 %shocks.1 = (bf16[64,1024]{1,0:T(8,128)(2,1)S(1)}, s32[64,8,128]{2,1,0:T(8,128)S(1)}, bf16[200,1024]{1,0:T(8,128)(2,1)S(1)}, s32[1,200]{1,0:T(1,128)S(1)}, s32[16]{0:T(128)S(4)}) custom-call(bf16[1000,1024]{1,0:T(8,128)(2,1)} %bitcast.7, bf16[64,1000]{1,0:T(8,128)(2,1)} %bitcast.10, s32[64,8,128]{2,1,0:T(8,128)} %bitcast.9, bf16[200,1024]{1,0:T(8,128)(2,1)} %bitcast.8, ...), custom_call_target="tpu_custom_call" | custom-call | tf_op jit(solution)/shard_map/shocks/pallas_call | solution.py:332
  3.0 0.1 collective-permute-start
  3.1 4.2 %collective-permute-start.1 = (bf16[64,1024]{1,0:T(8,128)(2,1)S(1)}, bf16[64,1024]{1,0:T(8,128)(2,1)S(1)}, u32[]{:S(2)}, u32[]{:S(2)}) collective-permute-start(bf16[64,1024]{1,0:T(8,128)(2,1)S(1)} %get-tuple-element.16.own), channel_id=1, source_target_pairs={{1,2},{2,1},{3,4},{4,3},{5,6},{6,5},{7,8},{8,7},{9,10},{10,9},{11,... | collective-permute-start | bytes 393224 | tf_op jit(solution)/shard_map/ppermute | solution.py:363
  7.3 0.1 collective-permute-start.2
  7.4 3.2 %collective-permute-start.3 = (bf16[64,1024]{1,0:T(8,128)(2,1)S(1)}, bf16[64,1024]{1,0:T(8,128)(2,1)S(1)}, u32[]{:S(2)}, u32[]{:S(2)}) collective-permute-start(bf16[64,1024]{1,0:T(8,128)(2,1)S(1)} %get-tuple-element.16.own), channel_id=1, source_target_pairs={{2,4},{3,5},{4,2},{5,3},{6,8},{7,9},{8,6},{9,7},{10,12},{11,13},{1... | collective-permute-start | bytes 393224 | tf_op jit(solution)/shard_map/ppermute | solution.py:363
  10.6 2.7 %delta.1 = (f32[64,8,256]{2,1,0:T(8,128)S(1)}, s16[64,16,128]{2,1,0:T(8,128)(2,1)S(1)}, bf16[2,1024,1024]{2,1,0:T(8,128)(2,1)S(1)}) custom-call(bf16[64,1024]{1,0:T(8,128)(2,1)S(1)} %get-tuple-element.16.own, s32[64,8,128]{2,1,0:T(8,128)S(1)} %get-tuple-element.17.buckets, bf16[200,1024]{1,0:T(8,128)(2,1)S(1)} %get-tuple-element.19.sens_t, ...), custom_call_target="tpu_custom_call" | custom-call | tf_op jit(solution)/shard_map/delta/pallas_call | solution.py:366
  13.3 0.0 collective-permute-done.near
  13.3 0.0 collective-permute-done.1.far
  13.3 0.0 collective-permute-done.2.chip_near
  13.3 1.6 %collective-permute-done.3.chip_far = bf16[64,1024]{1,0:T(8,128)(2,1)S(1)} collective-permute-done((bf16[64,1024]{1,0:T(8,128)(2,1)S(1)}, bf16[64,1024]{1,0:T(8,128)(2,1)S(1)}, u32[]{:S(2)}, u32[]{:S(2)}) %collective-permute-start.3) | collective-permute-done | bytes 131104 | tf_op jit(solution)/shard_map/ppermute | solution.py:363
  15.0 1.1 %gamma.1 = s16[64,16,128]{2,1,0:T(8,128)(2,1)S(1)} custom-call(s32[16]{0:T(128)S(4)} %get-tuple-element.15.meta, bf16[64,1024]{1,0:T(8,128)(2,1)S(1)} %get-tuple-element.16.own, bf16[64,1024]{1,0:T(8,128)(2,1)S(1)} %collective-permute-done.near, bf16[64,1024]{1,0:T(8,128)(2,1)S(1)} %collective-permute-done.1.far, ...), custom_call_target="tpu_custom_call", output_to_operand_aliasing={{}: (10, {})} | custom-call | tf_op jit(solution)/shard_map/gamma/pallas_call | solution.py:377
  16.0 26.1 %all_to_all.5.received = s16[64,16,128]{2,1,0:T(8,128)(2,1)S(1)} all-to-all(s16[64,16,128]{2,1,0:T(8,128)(2,1)S(1)} %gamma.1), channel_id=1, replica_groups=mesh['scen'=4,'fac'=64] {'fac'}, dimensions={0} | all-to-all | bytes 524288 | tf_op jit(solution)/shard_map/all_to_all | solution.py:387
  42.2 0.8 %total.1 = (f32[40,128]{1,0:T(8,128)S(1)}, f32[5,5,64]{2,1,0:T(8,128)}) custom-call(s16[64,16,128]{2,1,0:T(8,128)(2,1)S(1)} %all_to_all.5.received), custom_call_target="tpu_custom_call" | custom-call | tf_op jit(solution)/shard_map/total/pallas_call | solution.py:388
  43.0 1.6 %collective-permute-start.4 = (f32[40,128]{1,0:T(8,128)S(1)}, f32[40,128]{1,0:T(8,128)S(1)}, u32[]{:S(2)}, u32[]{:S(2)}) collective-permute-start(f32[40,128]{1,0:T(8,128)S(1)} %get-tuple-element.24.own), channel_id=1, source_target_pairs={{0,64},{64,0},{128,192},{192,128},{1,65},{65,1},{129,193},{193,129... | collective-permute-start | bytes 61448 | tf_op jit(solution)/shard_map/ppermute | solution.py:400
  44.5 2.2 %collective-permute-start.5 = (f32[40,128]{1,0:T(8,128)S(1)}, f32[40,128]{1,0:T(8,128)S(1)}, u32[]{:S(2)}, u32[]{:S(2)}) collective-permute-start(f32[40,128]{1,0:T(8,128)S(1)} %get-tuple-element.24.own), channel_id=1, source_target_pairs={{0,192},{64,128},{128,64},{192,0},{1,193},{65,129},{129,65},{193,1... | collective-permute-start | bytes 61448 | tf_op jit(solution)/shard_map/ppermute | solution.py:400
  46.7 0.7 %collective-permute-start.6 = (f32[40,128]{1,0:T(8,128)S(1)}, f32[40,128]{1,0:T(8,128)S(1)}, u32[]{:S(2)}, u32[]{:S(2)}) collective-permute-start(f32[40,128]{1,0:T(8,128)S(1)} %get-tuple-element.24.own), channel_id=1, source_target_pairs={{0,128},{64,192},{128,0},{192,64},{1,129},{65,193},{129,1},{193,65... | collective-permute-start | bytes 61448 | tf_op jit(solution)/shard_map/ppermute | solution.py:400
  47.5 0.0 collective-permute-done.4.other1
  47.5 2.1 %collective-permute-done.5.other2 = f32[40,128]{1,0:T(8,128)S(1)} collective-permute-done((f32[40,128]{1,0:T(8,128)S(1)}, f32[40,128]{1,0:T(8,128)S(1)}, u32[]{:S(2)}, u32[]{:S(2)}) %collective-permute-start.5) | collective-permute-done | bytes 20512 | tf_op jit(solution)/shard_map/ppermute | solution.py:400
  49.5 2.5 %collective-permute-done.6.other3 = f32[40,128]{1,0:T(8,128)S(1)} collective-permute-done((f32[40,128]{1,0:T(8,128)S(1)}, f32[40,128]{1,0:T(8,128)S(1)}, u32[]{:S(2)}, u32[]{:S(2)}) %collective-permute-start.6) | collective-permute-done | bytes 20512 | tf_op jit(solution)/shard_map/ppermute | solution.py:400
  52.0 1.1 %tail.1 = (f32[5,5]{1,0:T(8,128)}, f32[1,5]{1,0:T(1,128)}) custom-call(f32[40,128]{1,0:T(8,128)S(1)} %get-tuple-element.24.own, f32[40,128]{1,0:T(8,128)S(1)} %collective-permute-done.4.other1, f32[40,128]{1,0:T(8,128)S(1)} %collective-permute-done.5.other2, f32[40,128]{1,0:T(8,128)S(1)} %collective-permute-done.6.other3), custom_call_target="tpu_custom_call" | custom-call | tf_op jit(solution)/shard_map/tail/pallas_call | solution.py:403
Async XLA Ops:
  3.0 10.3 %collective-permute-start = (bf16[64,1024]{1,0:T(8,128)(2,1)S(1)}, bf16[64,1024]{1,0:T(8,128)(2,1)S(1)}, u32[]{:S(2)}, u32[]{:S(2)}) collective-permute-start(bf16[64,1024]{1,0:T(8,128)(2,1)S(1)} %get-tuple-element.16.own), channel_id=1, source_target_pairs={{0,1},{1,0},{2,3},{3,2},{4,5},{5,4},{6,7},{7,6},{8,9},{9,8},{10,11... | collective-permute-start | bytes 393224 | tf_op jit(solution)/shard_map/ppermute | solution.py:363
  3.1 10.3 %collective-permute-start.1 = (bf16[64,1024]{1,0:T(8,128)(2,1)S(1)}, bf16[64,1024]{1,0:T(8,128)(2,1)S(1)}, u32[]{:S(2)}, u32[]{:S(2)}) collective-permute-start(bf16[64,1024]{1,0:T(8,128)(2,1)S(1)} %get-tuple-element.16.own), channel_id=1, source_target_pairs={{1,2},{2,1},{3,4},{4,3},{5,6},{6,5},{7,8},{8,7},{9,10},{10,9},{11,... | collective-permute-start | bytes 393224 | tf_op jit(solution)/shard_map/ppermute | solution.py:363
  7.3 6.0 %collective-permute-start.2 = (bf16[64,1024]{1,0:T(8,128)(2,1)S(1)}, bf16[64,1024]{1,0:T(8,128)(2,1)S(1)}, u32[]{:S(2)}, u32[]{:S(2)}) collective-permute-start(bf16[64,1024]{1,0:T(8,128)(2,1)S(1)} %get-tuple-element.16.own), channel_id=1, source_target_pairs={{0,2},{1,3},{2,0},{3,1},{4,6},{5,7},{6,4},{7,5},{8,10},{9,11},{10,... | collective-permute-start | bytes 393224 | tf_op jit(solution)/shard_map/ppermute | solution.py:363
  7.4 7.6 %collective-permute-start.3 = (bf16[64,1024]{1,0:T(8,128)(2,1)S(1)}, bf16[64,1024]{1,0:T(8,128)(2,1)S(1)}, u32[]{:S(2)}, u32[]{:S(2)}) collective-permute-start(bf16[64,1024]{1,0:T(8,128)(2,1)S(1)} %get-tuple-element.16.own), channel_id=1, source_target_pairs={{2,4},{3,5},{4,2},{5,3},{6,8},{7,9},{8,6},{9,7},{10,12},{11,13},{1... | collective-permute-start | bytes 393224 | tf_op jit(solution)/shard_map/ppermute | solution.py:363
  43.0 4.5 %collective-permute-start.4 = (f32[40,128]{1,0:T(8,128)S(1)}, f32[40,128]{1,0:T(8,128)S(1)}, u32[]{:S(2)}, u32[]{:S(2)}) collective-permute-start(f32[40,128]{1,0:T(8,128)S(1)} %get-tuple-element.24.own), channel_id=1, source_target_pairs={{0,64},{64,0},{128,192},{192,128},{1,65},{65,1},{129,193},{193,129... | collective-permute-start | bytes 61448 | tf_op jit(solution)/shard_map/ppermute | solution.py:400
  44.5 5.0 %collective-permute-start.5 = (f32[40,128]{1,0:T(8,128)S(1)}, f32[40,128]{1,0:T(8,128)S(1)}, u32[]{:S(2)}, u32[]{:S(2)}) collective-permute-start(f32[40,128]{1,0:T(8,128)S(1)} %get-tuple-element.24.own), channel_id=1, source_target_pairs={{0,192},{64,128},{128,64},{192,0},{1,193},{65,129},{129,65},{193,1... | collective-permute-start | bytes 61448 | tf_op jit(solution)/shard_map/ppermute | solution.py:400
  46.7 5.3 %collective-permute-start.6 = (f32[40,128]{1,0:T(8,128)S(1)}, f32[40,128]{1,0:T(8,128)S(1)}, u32[]{:S(2)}, u32[]{:S(2)}) collective-permute-start(f32[40,128]{1,0:T(8,128)S(1)} %get-tuple-element.24.own), channel_id=1, source_target_pairs={{0,128},{64,192},{128,0},{192,64},{1,129},{65,193},{129,1},{193,65... | collective-permute-start | bytes 61448 | tf_op jit(solution)/shard_map/ppermute | solution.py:400

commit v3 on v2

--- a/solution.py
+++ b/solution.py
@@ -303,7 +303,8 @@
 VMEM = pl.BlockSpec(memory_space=pltpu.VMEM)
 SMEM = pl.BlockSpec(memory_space=pltpu.SMEM)
 HBM = pl.BlockSpec(memory_space=pltpu.HBM)
-ORDER = (0, 2, 1, 3)
+ORDER = (3, 1, 2, 0)
+SCEN_ORDER = (2, 3, 1)
 
 
 def held(value):
@@ -360,7 +361,9 @@
         )
     )
     pairs = swap_pairs(fac_count)
-    moved = {index: held(lax.ppermute(shocks, "fac", pairs[index])) for index in ORDER}
+    moved = {}
+    for index in ORDER:
+        moved[index] = held(lax.ppermute(shocks, "fac", pairs[index]))
     chunk_shape = (fac_count, ROWS, LANES)
     coded_shape = pltpu.VMEM((fac_count, 2 * ROWS, LANES // 2), jnp.int16)
     delta, coded, gamma = pl.pallas_call(
@@ -396,10 +399,9 @@
         name="total",
         compiler_params=limited(8),
     )(received)
-    others = [
-        held(lax.ppermute(packed, "scen", [(i, i ^ step) for i in range(scen_count)]))
-        for step in (1, 3, 2)
-    ]
+    others = []
+    for step in SCEN_ORDER:
+        others.append(held(lax.ppermute(packed, "scen", [(i, i ^ step) for i in range(scen_count)])))
     shortfall, adjusted = pl.pallas_call(
         tail_kernel,
         out_shape=(

time: 53.3 us -> 53 us (level)
  Pallas kernels: 8.05 us -> 9.11 us
  blocking collectives: 26.1 us -> 25.1 us
  waiting for transfers between devices: 6.21 us -> 5.58 us
    pallas_call x1, Pallas kernels: 1.07 us -> 2.12 us  [local(): pl.pallas_call(gamma_kernel, out_shape=coded_shape, in_specs=[SMEM] + [VM...]
    all_to_all x1, blocking collectives: 26.1 us -> 25.1 us  [local(): received = held(lax.all_to_all(terms, 'fac', 0, 0, tiled=False))]
    ppermute x3, waiting for transfers between devices: 4.56 us -> 3.94 us  [local(): lax.ppermute(packed, 'scen', [(i, i ^ step) for i in range(scen_count)])]
where the time goes in v3:
time: 53 us; the launch traced here: 52.3 us
  blocking collectives  25.1 us (47%)
  starting transfers between devices  11.8 us (22%)
  Pallas kernels  9.11 us (17%)
  waiting for transfers between devices  5.58 us (11%)
  between operations  0.72 us (1%)
    all_to_all x1, blocking collectives, local(): received = held(lax.all_to_all(terms, 'fac', 0, 0, tiled=False))  25.1 us
    ppermute x4, starting transfers between devices, local(): moved[index] = held(lax.ppermute(shocks, 'fac', pairs[index]))  7.58 us
    ppermute x3, starting transfers between devices, local(): lax.ppermute(packed, 'scen', [(i, i ^ step) for i in range(scen_count)])  4.25 us
    ppermute x3, waiting for transfers between devices, local(): lax.ppermute(packed, 'scen', [(i, i ^ step) for i in range(scen_count)])  3.94 us
    pallas_call x1, Pallas kernels, local(): pl.pallas_call(delta_kernel, out_shape=(pltpu.VMEM(chunk_shape, f32), cod...  2.72 us
    pallas_call x1, Pallas kernels, local(): pl.pallas_call(shocks_kernel, out_shape=(pltpu.VMEM((s_dev, BLK), bf16),...  2.32 us
    pallas_call x1, Pallas kernels, local(): pl.pallas_call(gamma_kernel, out_shape=coded_shape, in_specs=[SMEM] + [VM...  2.12 us
    ppermute x4, waiting for transfers between devices, local(): moved[index] = held(lax.ppermute(shocks, 'fac', pairs[index]))  1.64 us
  transfers between devices with their start and end apart: 7, of which 3 were waited for; matrix products, arithmetic and copies ran while one was open for 0% of the time, Pallas kernels for 5%

profile of v3, /device:TPU:2, one launch (start us, length us, event | category | flops | bytes accessed | tf_op | source)
XLA Modules:
  0.0 52.3 jit_solution(11063830990737860359)
XLA Ops:
  0.6 2.3 %shocks.1 = (bf16[64,1024]{1,0:T(8,128)(2,1)S(1)}, s32[64,8,128]{2,1,0:T(8,128)S(1)}, bf16[200,1024]{1,0:T(8,128)(2,1)S(1)}, s32[1,200]{1,0:T(1,128)S(1)}, s32[16]{0:T(128)S(4)}) custom-call(bf16[1000,1024]{1,0:T(8,128)(2,1)} %bitcast.7, bf16[64,1000]{1,0:T(8,128)(2,1)} %bitcast.10, s32[64,8,128]{2,1,0:T(8,128)} %bitcast.9, bf16[200,1024]{1,0:T(8,128)(2,1)} %bitcast.8, ...), custom_call_target="tpu_custom_call" | custom-call | tf_op jit(solution)/shard_map/shocks/pallas_call | solution.py:333
  3.0 0.1 collective-permute-start
  3.1 4.2 %collective-permute-start.1 = (bf16[64,1024]{1,0:T(8,128)(2,1)S(1)}, bf16[64,1024]{1,0:T(8,128)(2,1)S(1)}, u32[]{:S(2)}, u32[]{:S(2)}) collective-permute-start(bf16[64,1024]{1,0:T(8,128)(2,1)S(1)} %get-tuple-element.16.own), channel_id=1, source_target_pairs={{1,2},{2,1},{3,4},{4,3},{5,6},{6,5},{7,8},{8,7},{9,10},{10,9},{11,... | collective-permute-start | bytes 393224 | tf_op jit(solution)/shard_map/ppermute | solution.py:366
  7.3 0.1 collective-permute-start.2
  7.4 3.2 %collective-permute-start.3 = (bf16[64,1024]{1,0:T(8,128)(2,1)S(1)}, bf16[64,1024]{1,0:T(8,128)(2,1)S(1)}, u32[]{:S(2)}, u32[]{:S(2)}) collective-permute-start(bf16[64,1024]{1,0:T(8,128)(2,1)S(1)} %get-tuple-element.16.own), channel_id=1, source_target_pairs={{2,4},{3,5},{4,2},{5,3},{6,8},{7,9},{8,6},{9,7},{10,12},{11,13},{1... | collective-permute-start | bytes 393224 | tf_op jit(solution)/shard_map/ppermute | solution.py:366
  10.6 2.7 %delta.1 = (f32[64,8,256]{2,1,0:T(8,128)S(1)}, s16[64,16,128]{2,1,0:T(8,128)(2,1)S(1)}, bf16[2,1024,1024]{2,1,0:T(8,128)(2,1)S(1)}) custom-call(bf16[64,1024]{1,0:T(8,128)(2,1)S(1)} %get-tuple-element.16.own, s32[64,8,128]{2,1,0:T(8,128)S(1)} %get-tuple-element.17.buckets, bf16[200,1024]{1,0:T(8,128)(2,1)S(1)} %get-tuple-element.19.sens_t, ...), custom_call_target="tpu_custom_call" | custom-call | tf_op jit(solution)/shard_map/delta/pallas_call | solution.py:369
  13.3 0.0 collective-permute-done.near
  13.3 0.0 collective-permute-done.1.far
  13.3 0.0 collective-permute-done.2.chip_near
  13.3 1.6 %collective-permute-done.3.chip_far = bf16[64,1024]{1,0:T(8,128)(2,1)S(1)} collective-permute-done((bf16[64,1024]{1,0:T(8,128)(2,1)S(1)}, bf16[64,1024]{1,0:T(8,128)(2,1)S(1)}, u32[]{:S(2)}, u32[]{:S(2)}) %collective-permute-start.3) | collective-permute-done | bytes 131104 | tf_op jit(solution)/shard_map/ppermute | solution.py:366
  15.0 2.1 %gamma.1 = s16[64,16,128]{2,1,0:T(8,128)(2,1)S(1)} custom-call(s32[16]{0:T(128)S(4)} %get-tuple-element.15.meta, bf16[64,1024]{1,0:T(8,128)(2,1)S(1)} %get-tuple-element.16.own, bf16[64,1024]{1,0:T(8,128)(2,1)S(1)} %collective-permute-done.near, bf16[64,1024]{1,0:T(8,128)(2,1)S(1)} %collective-permute-done.1.far, ...), custom_call_target="tpu_custom_call", output_to_operand_aliasing={{}: (10, {})} | custom-call | tf_op jit(solution)/shard_map/gamma/pallas_call | solution.py:380
  17.1 25.1 %all_to_all.5.received = s16[64,16,128]{2,1,0:T(8,128)(2,1)S(1)} all-to-all(s16[64,16,128]{2,1,0:T(8,128)(2,1)S(1)} %gamma.1), channel_id=1, replica_groups=mesh['scen'=4,'fac'=64] {'fac'}, dimensions={0} | all-to-all | bytes 524288 | tf_op jit(solution)/shard_map/all_to_all | solution.py:390
  42.2 0.8 %total.1 = (f32[40,128]{1,0:T(8,128)S(1)}, f32[5,5,64]{2,1,0:T(8,128)}) custom-call(s16[64,16,128]{2,1,0:T(8,128)(2,1)S(1)} %all_to_all.5.received), custom_call_target="tpu_custom_call" | custom-call | tf_op jit(solution)/shard_map/total/pallas_call | solution.py:391
  43.0 3.2 %collective-permute-start.4 = (f32[40,128]{1,0:T(8,128)S(1)}, f32[40,128]{1,0:T(8,128)S(1)}, u32[]{:S(2)}, u32[]{:S(2)}) collective-permute-start(f32[40,128]{1,0:T(8,128)S(1)} %get-tuple-element.24.own), channel_id=1, source_target_pairs={{0,128},{64,192},{128,0},{192,64},{1,129},{65,193},{129,1},{193,65... | collective-permute-start | bytes 61448 | tf_op jit(solution)/shard_map/ppermute | solution.py:404
  46.2 1.1 %collective-permute-start.5 = (f32[40,128]{1,0:T(8,128)S(1)}, f32[40,128]{1,0:T(8,128)S(1)}, u32[]{:S(2)}, u32[]{:S(2)}) collective-permute-start(f32[40,128]{1,0:T(8,128)S(1)} %get-tuple-element.24.own), channel_id=1, source_target_pairs={{0,192},{64,128},{128,64},{192,0},{1,193},{65,129},{129,65},{193,1... | collective-permute-start | bytes 61448 | tf_op jit(solution)/shard_map/ppermute | solution.py:404
  47.3 0.0 collective-permute-start.6
  47.3 1.0 %collective-permute-done.4.other1 = f32[40,128]{1,0:T(8,128)S(1)} collective-permute-done((f32[40,128]{1,0:T(8,128)S(1)}, f32[40,128]{1,0:T(8,128)S(1)}, u32[]{:S(2)}, u32[]{:S(2)}) %collective-permute-start.4) | collective-permute-done | bytes 20512 | tf_op jit(solution)/shard_map/ppermute | solution.py:404
  48.3 2.9 %collective-permute-done.5.other2 = f32[40,128]{1,0:T(8,128)S(1)} collective-permute-done((f32[40,128]{1,0:T(8,128)S(1)}, f32[40,128]{1,0:T(8,128)S(1)}, u32[]{:S(2)}, u32[]{:S(2)}) %collective-permute-start.5) | collective-permute-done | bytes 20512 | tf_op jit(solution)/shard_map/ppermute | solution.py:404
  51.2 0.0 collective-permute-done.6.other3
  51.2 1.1 %tail.1 = (f32[5,5]{1,0:T(8,128)}, f32[1,5]{1,0:T(1,128)}) custom-call(f32[40,128]{1,0:T(8,128)S(1)} %get-tuple-element.24.own, f32[40,128]{1,0:T(8,128)S(1)} %collective-permute-done.4.other1, f32[40,128]{1,0:T(8,128)S(1)} %collective-permute-done.5.other2, f32[40,128]{1,0:T(8,128)S(1)} %collective-permute-done.6.other3), custom_call_target="tpu_custom_call" | custom-call | tf_op jit(solution)/shard_map/tail/pallas_call | solution.py:405
Async XLA Ops:
  3.0 10.3 %collective-permute-start = (bf16[64,1024]{1,0:T(8,128)(2,1)S(1)}, bf16[64,1024]{1,0:T(8,128)(2,1)S(1)}, u32[]{:S(2)}, u32[]{:S(2)}) collective-permute-start(bf16[64,1024]{1,0:T(8,128)(2,1)S(1)} %get-tuple-element.16.own), channel_id=1, source_target_pairs={{0,1},{1,0},{2,3},{3,2},{4,5},{5,4},{6,7},{7,6},{8,9},{9,8},{10,11... | collective-permute-start | bytes 393224 | tf_op jit(solution)/shard_map/ppermute | solution.py:366
  3.1 10.3 %collective-permute-start.1 = (bf16[64,1024]{1,0:T(8,128)(2,1)S(1)}, bf16[64,1024]{1,0:T(8,128)(2,1)S(1)}, u32[]{:S(2)}, u32[]{:S(2)}) collective-permute-start(bf16[64,1024]{1,0:T(8,128)(2,1)S(1)} %get-tuple-element.16.own), channel_id=1, source_target_pairs={{1,2},{2,1},{3,4},{4,3},{5,6},{6,5},{7,8},{8,7},{9,10},{10,9},{11,... | collective-permute-start | bytes 393224 | tf_op jit(solution)/shard_map/ppermute | solution.py:366
  7.3 6.0 %collective-permute-start.2 = (bf16[64,1024]{1,0:T(8,128)(2,1)S(1)}, bf16[64,1024]{1,0:T(8,128)(2,1)S(1)}, u32[]{:S(2)}, u32[]{:S(2)}) collective-permute-start(bf16[64,1024]{1,0:T(8,128)(2,1)S(1)} %get-tuple-element.16.own), channel_id=1, source_target_pairs={{0,2},{1,3},{2,0},{3,1},{4,6},{5,7},{6,4},{7,5},{8,10},{9,11},{10,... | collective-permute-start | bytes 393224 | tf_op jit(solution)/shard_map/ppermute | solution.py:366
  7.4 7.6 %collective-permute-start.3 = (bf16[64,1024]{1,0:T(8,128)(2,1)S(1)}, bf16[64,1024]{1,0:T(8,128)(2,1)S(1)}, u32[]{:S(2)}, u32[]{:S(2)}) collective-permute-start(bf16[64,1024]{1,0:T(8,128)(2,1)S(1)} %get-tuple-element.16.own), channel_id=1, source_target_pairs={{2,4},{3,5},{4,2},{5,3},{6,8},{7,9},{8,6},{9,7},{10,12},{11,13},{1... | collective-permute-start | bytes 393224 | tf_op jit(solution)/shard_map/ppermute | solution.py:366
  43.0 5.3 %collective-permute-start.4 = (f32[40,128]{1,0:T(8,128)S(1)}, f32[40,128]{1,0:T(8,128)S(1)}, u32[]{:S(2)}, u32[]{:S(2)}) collective-permute-start(f32[40,128]{1,0:T(8,128)S(1)} %get-tuple-element.24.own), channel_id=1, source_target_pairs={{0,128},{64,192},{128,0},{192,64},{1,129},{65,193},{129,1},{193,65... | collective-permute-start | bytes 61448 | tf_op jit(solution)/shard_map/ppermute | solution.py:404
  46.2 5.0 %collective-permute-start.5 = (f32[40,128]{1,0:T(8,128)S(1)}, f32[40,128]{1,0:T(8,128)S(1)}, u32[]{:S(2)}, u32[]{:S(2)}) collective-permute-start(f32[40,128]{1,0:T(8,128)S(1)} %get-tuple-element.24.own), channel_id=1, source_target_pairs={{0,192},{64,128},{128,64},{192,0},{1,193},{65,129},{129,65},{193,1... | collective-permute-start | bytes 61448 | tf_op jit(solution)/shard_map/ppermute | solution.py:404
  47.3 3.9 %collective-permute-start.6 = (f32[40,128]{1,0:T(8,128)S(1)}, f32[40,128]{1,0:T(8,128)S(1)}, u32[]{:S(2)}, u32[]{:S(2)}) collective-permute-start(f32[40,128]{1,0:T(8,128)S(1)} %get-tuple-element.24.own), channel_id=1, source_target_pairs={{0,64},{64,0},{128,192},{192,128},{1,65},{65,1},{129,193},{193,129... | collective-permute-start | bytes 61448 | tf_op jit(solution)/shard_map/ppermute | solution.py:404

commit v4 on v3

--- a/solution.py
+++ b/solution.py
@@ -18,18 +18,15 @@
 
 
 def swap_pairs(count):
-    near, far, chip_near, chip_far = [], [], [], []
+    near, chip_near, chip_far = [], [], []
     for index in range(count):
         near.append((index, index ^ 1))
-        other = ((index + 1) ^ 1) - 1
-        if 0 <= other < count:
-            far.append((index, other))
         chip, core = divmod(index, 2)
         chip_near.append((index, (chip ^ 1) * 2 + core))
         other = ((chip + 1) ^ 1) - 1
         if 0 <= other < count // 2:
             chip_far.append((index, other * 2 + core))
-    return near, far, chip_near, chip_far
+    return near, chip_near, chip_far
 
 
 def block_code(block, device):
@@ -303,7 +300,7 @@
 VMEM = pl.BlockSpec(memory_space=pltpu.VMEM)
 SMEM = pl.BlockSpec(memory_space=pltpu.SMEM)
 HBM = pl.BlockSpec(memory_space=pltpu.HBM)
-ORDER = (3, 1, 2, 0)
+ORDER = (2, 1, 0)
 SCEN_ORDER = (2, 3, 1)
 
 
@@ -363,7 +360,10 @@
     pairs = swap_pairs(fac_count)
     moved = {}
     for index in ORDER:
-        moved[index] = held(lax.ppermute(shocks, "fac", pairs[index]))
+        moved[index] = lax.ppermute(shocks, "fac", pairs[index])
+    device = lax.axis_index("fac")
+    onward = jnp.where((device % 2 == 0) == (device // 2 % 2 == 0), moved[1], moved[2])
+    far = held(lax.ppermute(onward, "fac", pairs[0]))
     chunk_shape = (fac_count, ROWS, LANES)
     coded_shape = pltpu.VMEM((fac_count, 2 * ROWS, LANES // 2), jnp.int16)
     delta, coded, gamma = pl.pallas_call(
@@ -386,7 +386,7 @@
         input_output_aliases={10: 0},
         name="gamma",
         compiler_params=limited(16),
-    )(meta, shocks, moved[0], moved[1], moved[2], moved[3], tiles, owner_row, gamma, delta, coded)
+    )(meta, shocks, held(moved[0]), far, held(moved[1]), held(moved[2]), tiles, owner_row, gamma, delta, coded)
     received = held(lax.all_to_all(terms, "fac", 0, 0, tiled=False))
     packed, profit = pl.pallas_call(
         sum_kernel,

time: 53 us -> 52.3 us (0.987)
  waiting for transfers between devices: 5.58 us -> 8.3 us
  starting transfers between devices: 11.8 us -> 9.11 us
  blocking collectives: 25.1 us -> 24.4 us
    ppermute x4, starting transfers between devices: 7.58 us -> 4.86 us  [the longest x3 4.76 us: local(): moved[index] = lax.ppermute(shocks, 'fac', pairs[index])]
    ppermute x4, waiting for transfers between devices: 1.64 us -> 4.36 us  [the longest x3 4.36 us: local(): moved[index] = lax.ppermute(shocks, 'fac', pairs[index])]
    all_to_all x1, blocking collectives: 25.1 us -> 24.4 us  [local(): received = held(lax.all_to_all(terms, 'fac', 0, 0, tiled=False))]
  transfers between devices with their start and end apart: 7 -> 7, of which waited for: 3 -> 4; matrix products, arithmetic and copies ran while one was open for 0% -> 0% of each run, Pallas kernels for 5% -> 5%
where the time goes in v4:
time: 52.3 us; the launch traced here: 51.7 us
  blocking collectives  24.4 us (47%)
  Pallas kernels  9.12 us (17%)
  starting transfers between devices  9.11 us (17%)
  waiting for transfers between devices  8.3 us (16%)
  between operations  0.74 us (1%)
    all_to_all x1, blocking collectives, local(): received = held(lax.all_to_all(terms, 'fac', 0, 0, tiled=False))  24.4 us
    ppermute x3, starting transfers between devices, local(): moved[index] = lax.ppermute(shocks, 'fac', pairs[index])  4.76 us
    ppermute x3, waiting for transfers between devices, local(): moved[index] = lax.ppermute(shocks, 'fac', pairs[index])  4.36 us
    ppermute x3, starting transfers between devices, local(): lax.ppermute(packed, 'scen', [(i, i ^ step) for i in range(scen_count)])  4.25 us
    ppermute x3, waiting for transfers between devices, local(): lax.ppermute(packed, 'scen', [(i, i ^ step) for i in range(scen_count)])  3.94 us
    pallas_call x1, Pallas kernels, local(): pl.pallas_call(delta_kernel, out_shape=(pltpu.VMEM(chunk_shape, f32), cod...  2.72 us
    pallas_call x1, Pallas kernels, local(): pl.pallas_call(shocks_kernel, out_shape=(pltpu.VMEM((s_dev, BLK), bf16),...  2.32 us
    pallas_call x1, Pallas kernels, local(): pl.pallas_call(gamma_kernel, out_shape=coded_shape, in_specs=[SMEM] + [VM...  2.13 us
  transfers between devices with their start and end apart: 7, of which 4 were waited for; matrix products, arithmetic and copies ran while one was open for 0% of the time, Pallas kernels for 5%

profile of v4, /device:TPU:2, one launch (start us, length us, event | category | flops | bytes accessed | tf_op | source)
XLA Modules:
  0.0 51.7 jit_solution(8106224762669692083)
XLA Ops:
  0.6 2.3 %shocks.1 = (bf16[64,1024]{1,0:T(8,128)(2,1)S(1)}, s32[64,8,128]{2,1,0:T(8,128)S(1)}, bf16[200,1024]{1,0:T(8,128)(2,1)S(1)}, s32[1,200]{1,0:T(1,128)S(1)}, s32[16]{0:T(128)S(4)}) custom-call(bf16[1000,1024]{1,0:T(8,128)(2,1)} %bitcast.7, bf16[64,1000]{1,0:T(8,128)(2,1)} %bitcast.10, s32[64,8,128]{2,1,0:T(8,128)} %bitcast.9, bf16[200,1024]{1,0:T(8,128)(2,1)} %bitcast.8, ...), custom_call_target="tpu_custom_call" | custom-call | tf_op jit(solution)/shard_map/shocks/pallas_call | solution.py:330
  3.0 2.3 %collective-permute-start.1 = (bf16[64,1024]{1,0:T(8,128)(2,1)S(1)}, bf16[64,1024]{1,0:T(8,128)(2,1)S(1)}, u32[]{:S(2)}, u32[]{:S(2)}) collective-permute-start(bf16[64,1024]{1,0:T(8,128)(2,1)S(1)} %get-tuple-element.16.own), channel_id=1, source_target_pairs={{0,2},{1,3},{2,0},{3,1},{4,6},{5,7},{6,4},{7,5},{8,10},{9,11},{10,... | collective-permute-start | bytes 393224 | tf_op jit(solution)/shard_map/ppermute | solution.py:363
  5.3 2.3 %collective-permute-start.2 = (bf16[64,1024]{1,0:T(8,128)(2,1)S(1)}, bf16[64,1024]{1,0:T(8,128)(2,1)S(1)}, u32[]{:S(2)}, u32[]{:S(2)}) collective-permute-start(bf16[64,1024]{1,0:T(8,128)(2,1)S(1)} %get-tuple-element.16.own), channel_id=1, source_target_pairs={{2,4},{3,5},{4,2},{5,3},{6,8},{7,9},{8,6},{9,7},{10,12},{11,13},{1... | collective-permute-start | bytes 393224 | tf_op jit(solution)/shard_map/ppermute | solution.py:363
  7.6 0.1 collective-permute-start
  7.8 0.5 collective-permute-done.1.chip_near
  8.3 3.9 %collective-permute-done.2.chip_far = bf16[64,1024]{1,0:T(8,128)(2,1)S(1)} collective-permute-done((bf16[64,1024]{1,0:T(8,128)(2,1)S(1)}, bf16[64,1024]{1,0:T(8,128)(2,1)S(1)}, u32[]{:S(2)}, u32[]{:S(2)}) %collective-permute-start.2) | collective-permute-done | bytes 131104 | tf_op jit(solution)/shard_map/ppermute | solution.py:363
  12.2 0.1 collective-permute-start.3
  12.3 2.7 %delta.1 = (f32[64,8,256]{2,1,0:T(8,128)S(1)}, s16[64,16,128]{2,1,0:T(8,128)(2,1)S(1)}, bf16[2,1024,1024]{2,1,0:T(8,128)(2,1)S(1)}) custom-call(bf16[64,1024]{1,0:T(8,128)(2,1)S(1)} %get-tuple-element.16.own, s32[64,8,128]{2,1,0:T(8,128)S(1)} %get-tuple-element.17.buckets, bf16[200,1024]{1,0:T(8,128)(2,1)S(1)} %get-tuple-element.19.sens_t, ...), custom_call_target="tpu_custom_call" | custom-call | tf_op jit(solution)/shard_map/delta/pallas_call | solution.py:369
  15.0 0.0 collective-permute-done.near
  15.0 0.0 collective-permute-done.3.far
  15.0 2.1 %gamma.1 = s16[64,16,128]{2,1,0:T(8,128)(2,1)S(1)} custom-call(s32[16]{0:T(128)S(4)} %get-tuple-element.15.meta, bf16[64,1024]{1,0:T(8,128)(2,1)S(1)} %get-tuple-element.16.own, bf16[64,1024]{1,0:T(8,128)(2,1)S(1)} %collective-permute-done.near, bf16[64,1024]{1,0:T(8,128)(2,1)S(1)} %collective-permute-done.3.far, ...), custom_call_target="tpu_custom_call", output_to_operand_aliasing={{}: (10, {})} | custom-call | tf_op jit(solution)/shard_map/gamma/pallas_call | solution.py:380
  17.1 24.4 %all_to_all.5.received = s16[64,16,128]{2,1,0:T(8,128)(2,1)S(1)} all-to-all(s16[64,16,128]{2,1,0:T(8,128)(2,1)S(1)} %gamma.1), channel_id=1, replica_groups=mesh['scen'=4,'fac'=64] {'fac'}, dimensions={0} | all-to-all | bytes 524288 | tf_op jit(solution)/shard_map/all_to_all | solution.py:390
  41.6 0.8 %total.1 = (f32[40,128]{1,0:T(8,128)S(1)}, f32[5,5,64]{2,1,0:T(8,128)}) custom-call(s16[64,16,128]{2,1,0:T(8,128)(2,1)S(1)} %all_to_all.5.received), custom_call_target="tpu_custom_call" | custom-call | tf_op jit(solution)/shard_map/total/pallas_call | solution.py:391
  42.4 3.2 %collective-permute-start.4 = (f32[40,128]{1,0:T(8,128)S(1)}, f32[40,128]{1,0:T(8,128)S(1)}, u32[]{:S(2)}, u32[]{:S(2)}) collective-permute-start(f32[40,128]{1,0:T(8,128)S(1)} %get-tuple-element.24.own), channel_id=1, source_target_pairs={{0,128},{64,192},{128,0},{192,64},{1,129},{65,193},{129,1},{193,65... | collective-permute-start | bytes 61448 | tf_op jit(solution)/shard_map/ppermute | solution.py:404
  45.6 1.1 %collective-permute-start.5 = (f32[40,128]{1,0:T(8,128)S(1)}, f32[40,128]{1,0:T(8,128)S(1)}, u32[]{:S(2)}, u32[]{:S(2)}) collective-permute-start(f32[40,128]{1,0:T(8,128)S(1)} %get-tuple-element.24.own), channel_id=1, source_target_pairs={{0,192},{64,128},{128,64},{192,0},{1,193},{65,129},{129,65},{193,1... | collective-permute-start | bytes 61448 | tf_op jit(solution)/shard_map/ppermute | solution.py:404
  46.6 0.0 collective-permute-start.6
  46.6 1.0 %collective-permute-done.4.other1 = f32[40,128]{1,0:T(8,128)S(1)} collective-permute-done((f32[40,128]{1,0:T(8,128)S(1)}, f32[40,128]{1,0:T(8,128)S(1)}, u32[]{:S(2)}, u32[]{:S(2)}) %collective-permute-start.4) | collective-permute-done | bytes 20512 | tf_op jit(solution)/shard_map/ppermute | solution.py:404
  47.7 2.9 %collective-permute-done.5.other2 = f32[40,128]{1,0:T(8,128)S(1)} collective-permute-done((f32[40,128]{1,0:T(8,128)S(1)}, f32[40,128]{1,0:T(8,128)S(1)}, u32[]{:S(2)}, u32[]{:S(2)}) %collective-permute-start.5) | collective-permute-done | bytes 20512 | tf_op jit(solution)/shard_map/ppermute | solution.py:404
  50.6 0.0 collective-permute-done.6.other3
  50.6 1.1 %tail.1 = (f32[5,5]{1,0:T(8,128)}, f32[1,5]{1,0:T(1,128)}) custom-call(f32[40,128]{1,0:T(8,128)S(1)} %get-tuple-element.24.own, f32[40,128]{1,0:T(8,128)S(1)} %collective-permute-done.4.other1, f32[40,128]{1,0:T(8,128)S(1)} %collective-permute-done.5.other2, f32[40,128]{1,0:T(8,128)S(1)} %collective-permute-done.6.other3), custom_call_target="tpu_custom_call" | custom-call | tf_op jit(solution)/shard_map/tail/pallas_call | solution.py:405
  (1 shorter events, 0.0 us)
Async XLA Ops:
  3.0 5.3 %collective-permute-start.1 = (bf16[64,1024]{1,0:T(8,128)(2,1)S(1)}, bf16[64,1024]{1,0:T(8,128)(2,1)S(1)}, u32[]{:S(2)}, u32[]{:S(2)}) collective-permute-start(bf16[64,1024]{1,0:T(8,128)(2,1)S(1)} %get-tuple-element.16.own), channel_id=1, source_target_pairs={{0,2},{1,3},{2,0},{3,1},{4,6},{5,7},{6,4},{7,5},{8,10},{9,11},{10,... | collective-permute-start | bytes 393224 | tf_op jit(solution)/shard_map/ppermute | solution.py:363
  5.3 6.8 %collective-permute-start.2 = (bf16[64,1024]{1,0:T(8,128)(2,1)S(1)}, bf16[64,1024]{1,0:T(8,128)(2,1)S(1)}, u32[]{:S(2)}, u32[]{:S(2)}) collective-permute-start(bf16[64,1024]{1,0:T(8,128)(2,1)S(1)} %get-tuple-element.16.own), channel_id=1, source_target_pairs={{2,4},{3,5},{4,2},{5,3},{6,8},{7,9},{8,6},{9,7},{10,12},{11,13},{1... | collective-permute-start | bytes 393224 | tf_op jit(solution)/shard_map/ppermute | solution.py:363
  7.6 7.3 %collective-permute-start = (bf16[64,1024]{1,0:T(8,128)(2,1)S(1)}, bf16[64,1024]{1,0:T(8,128)(2,1)S(1)}, u32[]{:S(2)}, u32[]{:S(2)}) collective-permute-start(bf16[64,1024]{1,0:T(8,128)(2,1)S(1)} %get-tuple-element.16.own), channel_id=1, source_target_pairs={{0,1},{1,0},{2,3},{3,2},{4,5},{5,4},{6,7},{7,6},{8,9},{9,8},{10,11... | collective-permute-start | bytes 393224 | tf_op jit(solution)/shard_map/ppermute | solution.py:363
  12.2 2.8 %collective-permute-start.3 = (bf16[64,1024]{1,0:T(8,128)(2,1)S(1)}, bf16[64,1024]{1,0:T(8,128)(2,1)S(1)}, u32[]{:S(2)}, u32[]{:S(2)}) collective-permute-start(bf16[64,1024]{1,0:T(8,128)(2,1)S(1)} %broadcast_select_fusion), channel_id=1, source_target_pairs={{0,1},{1,0},{2,3},{3,2},{4,5},{5,4},{6,7},{7,6},{8,9},{9,8},{10,11... | collective-permute-start | bytes 393224 | tf_op jit(solution)/shard_map/ppermute | solution.py:366
  42.4 5.3 %collective-permute-start.4 = (f32[40,128]{1,0:T(8,128)S(1)}, f32[40,128]{1,0:T(8,128)S(1)}, u32[]{:S(2)}, u32[]{:S(2)}) collective-permute-start(f32[40,128]{1,0:T(8,128)S(1)} %get-tuple-element.24.own), channel_id=1, source_target_pairs={{0,128},{64,192},{128,0},{192,64},{1,129},{65,193},{129,1},{193,65... | collective-permute-start | bytes 61448 | tf_op jit(solution)/shard_map/ppermute | solution.py:404
  45.6 5.0 %collective-permute-start.5 = (f32[40,128]{1,0:T(8,128)S(1)}, f32[40,128]{1,0:T(8,128)S(1)}, u32[]{:S(2)}, u32[]{:S(2)}) collective-permute-start(f32[40,128]{1,0:T(8,128)S(1)} %get-tuple-element.24.own), channel_id=1, source_target_pairs={{0,192},{64,128},{128,64},{192,0},{1,193},{65,129},{129,65},{193,1... | collective-permute-start | bytes 61448 | tf_op jit(solution)/shard_map/ppermute | solution.py:404
  46.6 3.9 %collective-permute-start.6 = (f32[40,128]{1,0:T(8,128)S(1)}, f32[40,128]{1,0:T(8,128)S(1)}, u32[]{:S(2)}, u32[]{:S(2)}) collective-permute-start(f32[40,128]{1,0:T(8,128)S(1)} %get-tuple-element.24.own), channel_id=1, source_target_pairs={{0,64},{64,0},{128,192},{192,128},{1,65},{65,1},{129,193},{193,129... | collective-permute-start | bytes 61448 | tf_op jit(solution)/shard_map/ppermute | solution.py:404

commit v5 on v4

--- a/solution.py
+++ b/solution.py
@@ -13,6 +13,7 @@
 LANES = 256
 TAIL = 7
 CHUNKS = 4
+FAR = 2
 
 horizon_weights = (1.0, 1.0, 2.0, 2.0, 6.0)
 
@@ -39,9 +40,8 @@
 
 
 def shocks_kernel(
-    loadings_t, reduced_t, tiles_hbm, sens_hbm, owner_hbm, block_owner_hbm, block_list_hbm,
-    desk_owner_hbm, shocks, tiles, sens_t, owner_row, meta, weights, factors, block_owner,
-    block_list, desk_owner, sems,
+    loadings_t, reduced_t, tiles_hbm, owner_hbm, block_owner_hbm, block_list_hbm, desk_owner_hbm,
+    shocks, tiles, owner_row, meta, weights, factors, block_owner, block_list, desk_owner, sems,
 ):
     parts = CHUNKS
     span = BLK // parts
@@ -56,11 +56,7 @@
         pltpu.make_async_copy(block_list_hbm, block_list, sems.at[parts + 2]),
         pltpu.make_async_copy(desk_owner_hbm, desk_owner, sems.at[parts + 3]),
     ]
-    later = [
-        pltpu.make_async_copy(owner_hbm, owner_row, sems.at[parts + 4]),
-        pltpu.make_async_copy(tiles_hbm, tiles, sems.at[parts + 5]),
-        pltpu.make_async_copy(sens_hbm, sens_t, sems.at[parts + 6]),
-    ]
+    later = [pltpu.make_async_copy(owner_hbm, owner_row, sems.at[parts + 4])]
     for copy in scalars + copies + later:
         copy.start()
     for copy in scalars:
@@ -75,16 +71,20 @@
         first = jnp.where(hit, block, first)
         live = live + jnp.where(hit, 1, 0)
     meta[0] = live
+    sources = [device]
     for slot, block in enumerate((first, second)):
         row = block_list[0, block]
         col = block_list[1, block]
         desk = block_list[2, block]
-        meta[1 + 6 * slot] = row
         meta[2 + 6 * slot] = block_code(row, device)
-        meta[3 + 6 * slot] = col
         meta[4 + 6 * slot] = block_code(col, device)
         meta[5 + 6 * slot] = desk
         meta[6 + 6 * slot] = desk_owner[desk]
+        sources += [row, col]
+    for index, block in enumerate(sources):
+        copy = pltpu.make_async_copy(tiles_hbm.at[block], tiles.at[index], sems.at[parts + 5 + index])
+        copy.start()
+        later.append(copy)
     copies[0].wait()
     for part in range(parts):
         copies[1 + part].wait()
@@ -131,13 +131,16 @@
     return value.astype(jnp.int32).astype(jnp.int16)
 
 
-def delta_kernel(own, buckets, sens_t, owner_row_ref, gamma_hbm, out, coded, gamma, sem):
-    copy = pltpu.make_async_copy(gamma_hbm, gamma, sem)
+def delta_kernel(
+    own, tiles, owner_row_ref, sens_hbm, gamma_hbm, out, coded, gamma, sens_t, sems
+):
+    sens_copy = pltpu.make_async_copy(sens_hbm, sens_t, sems.at[0])
+    copy = pltpu.make_async_copy(gamma_hbm, gamma, sems.at[1])
+    sens_copy.start()
     copy.start()
     desks = sens_t.shape[0]
     fac_count = out.shape[0]
     count = fac_count * ROWS
-    device = lax.axis_index("fac")
     owner_row = owner_row_ref[...]
     groups = lax.broadcasted_iota(jnp.int32, (fac_count, desks), 0)
     member = jnp.where(groups == jnp.broadcast_to(owner_row, (fac_count, desks)), 1.0, 0.0)
@@ -159,10 +162,11 @@
         1.0,
         0.0,
     ).astype(jnp.bfloat16)
+    masked = masked_rows(own[...], tiles[0])
+    sens_copy.wait()
     placed = lax.dot_general(
         placement, sens_t[...], (((1,), (0,)), ((), ())), preferred_element_type=jnp.float32
     ).astype(jnp.bfloat16)
-    masked = masked_rows(own[...], buckets[device])
     delta = lax.dot_general(
         placed, masked, (((1,), (1,)), ((), ())), preferred_element_type=jnp.float32
     )
@@ -173,32 +177,73 @@
     copy.wait()
 
 
+def picked(code, tile, own, others):
+    value = own[...]
+    for index, ref in others:
+        value = jnp.where(code == index, ref[...], value)
+    return masked_rows(value, tile)
+
+
+def early_kernel(meta, own, near, chip_near, chip_far, tiles, gamma, product):
+    others = ((1, near), (3, chip_near), (4, chip_far))
+    for slot in range(CAP):
+        row_code = meta[2 + 6 * slot]
+        col_code = meta[4 + 6 * slot]
+        live = slot < meta[0]
+
+        @pl.when(jnp.logical_and(live, row_code != FAR))
+        def _(slot=slot, row_code=row_code):
+            part = picked(row_code, tiles[1 + 2 * slot], own, others)
+            product[slot] = lax.dot_general(
+                part, gamma[slot], (((1,), (0,)), ((), ())), preferred_element_type=jnp.float32
+            )
+
+        late = jnp.logical_and(row_code == FAR, col_code != FAR)
+
+        @pl.when(jnp.logical_and(live, late))
+        def _(slot=slot, col_code=col_code):
+            part = picked(col_code, tiles[2 + 2 * slot], own, others)
+            product[slot] = lax.dot_general(
+                part, gamma[slot], (((1,), (1,)), ((), ())), preferred_element_type=jnp.float32
+            )
+
+
 def gamma_kernel(
-    meta, own, near, far, chip_near, chip_far, buckets, owner_row_ref, gamma, delta, coded, out, sums,
+    meta, own, near, far, chip_near, chip_far, tiles, owner_row_ref, gamma, product, delta, coded,
+    out, sums, quads,
 ):
     del coded
     desks = owner_row_ref.shape[1]
     width = HORIZONS * own.shape[0]
     live = meta[0]
     sums[...] = jnp.zeros(sums.shape, jnp.float32)
-
-    def pick(block, code):
-        value = own[...]
-        for index, ref in ((1, near), (2, far), (3, chip_near), (4, chip_far)):
-            value = jnp.where(code == index, ref[...], value)
-        return masked_rows(value, buckets[block])
+    others = ((1, near), (FAR, far), (3, chip_near), (4, chip_far))
 
     for slot in range(CAP):
         @pl.when(slot < live)
         def _(slot=slot):
-            row_part = pick(meta[1 + 6 * slot], meta[2 + 6 * slot])
-            col_part = pick(meta[3 + 6 * slot], meta[4 + 6 * slot])
+            row_code = meta[2 + 6 * slot]
+            col_code = meta[4 + 6 * slot]
             desk = meta[5 + 6 * slot]
             owner = meta[6 + 6 * slot]
-            product = lax.dot_general(
-                row_part, gamma[slot], (((1,), (0,)), ((), ())), preferred_element_type=jnp.float32
-            )
-            quad = 0.5 * jnp.sum(col_part.astype(jnp.float32) * product, axis=1, keepdims=True)
+            use_row = row_code == FAR
+            tile = jnp.where(use_row, tiles[1 + 2 * slot], tiles[2 + 2 * slot])
+            part = picked(jnp.where(use_row, row_code, col_code), tile, own, others)
+            whole = part.astype(jnp.float32)
+            both = jnp.logical_and(use_row, col_code == FAR)
+
+            @pl.when(both)
+            def _():
+                value = lax.dot_general(
+                    part, gamma[slot], (((1,), (0,)), ((), ())), preferred_element_type=jnp.float32
+                )
+                quads[...] = jnp.sum(whole * value, axis=1, keepdims=True)
+
+            @pl.when(jnp.logical_not(both))
+            def _():
+                quads[...] = jnp.sum(whole * product[slot], axis=1, keepdims=True)
+
+            quad = 0.5 * quads[...]
             diagonal = lax.broadcasted_iota(jnp.int32, (width, width), 0) == lax.broadcasted_iota(
                 jnp.int32, (width, width), 1
             )
@@ -240,7 +285,7 @@
         out[second] = encoded(two[None])[0]
 
 
-def sum_kernel(received, packed, profit):
+def sum_kernel(received, packed):
     lanes = 128
     value = received[...].astype(jnp.int32).astype(jnp.float32)
     value = value.reshape(received.shape[0] * 2, ROWS, lanes)
@@ -257,20 +302,30 @@
     ):
         moved = pltpu.roll(source, ROWS - shift, 0)
         fifth = jnp.where(row == j, moved, fifth)
-    for h, block in enumerate((low, low_turned, high, high_turned, fifth)):
-        packed[ROWS * h : ROWS * h + ROWS, :] = block
+    packed[...] = jnp.concatenate([low, high, fifth], axis=0)
+
+
+def profit_kernel(packed, profit):
+    for h in range(HORIZONS):
+        start = 64 * (h % 2)
+        block = packed[ROWS * (h // 2) : ROWS * (h // 2) + ROWS, start : start + 64]
         for j in range(DESK_DEV):
-            profit[j, h : h + 1, :] = block[j : j + 1, :64]
+            profit[j, h : h + 1, :] = block[j : j + 1, :]
 
 
 def tail_kernel(own, other1, other2, other3, shortfall, adjusted):
     lanes = 128
     count = HORIZONS * ROWS
-    lane = lax.broadcasted_iota(jnp.int32, (count, lanes), 1)
+    lower = lax.broadcasted_iota(jnp.int32, (3 * ROWS, lanes), 1) < 64
     filler = jnp.zeros((lanes - count, lanes), jnp.float32)
     columns = []
     for one, two in ((own, other1), (other2, other3)):
-        pair = -jnp.where(lane < 64, one[...], pltpu.roll(two[...], 64, 1))
+        even = jnp.where(lower, one[...], pltpu.roll(two[...], 64, 1))
+        odd = jnp.where(lower, pltpu.roll(one[...], 64, 1), two[...])
+        pair = -jnp.concatenate(
+            [even[:ROWS], odd[:ROWS], even[ROWS : 2 * ROWS], odd[ROWS : 2 * ROWS], even[2 * ROWS :]],
+            axis=0,
+        )
         columns.append(jnp.transpose(jnp.concatenate([pair, filler], axis=0)))
     values = jnp.concatenate(columns, axis=0).reshape(32, 8, lanes)
     total = jnp.zeros((1, lanes), jnp.float32)
@@ -327,24 +382,23 @@
     bf16 = jnp.bfloat16
     i32 = jnp.int32
     tile_shape = (fac_count, 8, BLK // 8)
-    shocks, tiles, sens_t, owner_row, meta = pl.pallas_call(
+    shocks, tiles, owner_row, meta = pl.pallas_call(
         shocks_kernel,
         out_shape=(
             pltpu.VMEM((s_dev, BLK), bf16),
-            pltpu.VMEM(tile_shape, i32),
-            pltpu.VMEM((desks, BLK), bf16),
+            pltpu.VMEM((1 + 2 * CAP, *tile_shape[1:]), i32),
             pltpu.VMEM((1, desks), i32),
             pltpu.SMEM((16,), i32),
         ),
-        in_specs=[HBM] * 8,
-        out_specs=(VMEM, VMEM, VMEM, VMEM, SMEM),
+        in_specs=[HBM] * 7,
+        out_specs=(VMEM, VMEM, VMEM, SMEM),
         scratch_shapes=[
             pltpu.VMEM((factors, BLK), bf16),
             pltpu.VMEM((s_dev, factors), bf16),
             pltpu.SMEM(block_owner.shape, i32),
             pltpu.SMEM(block_list.shape[::-1], i32),
             pltpu.SMEM(desk_owner.shape, i32),
-            pltpu.SemaphoreType.DMA((CHUNKS + 7,)),
+            pltpu.SemaphoreType.DMA((CHUNKS + 6 + 2 * CAP,)),
         ],
         name="shocks",
         compiler_params=limited(10),
@@ -352,7 +406,7 @@
         *map(
             resident,
             (
-                loadings.T, reduced_shocks.T, buckets.reshape(tile_shape), sensitivity.T,
+                loadings.T, reduced_shocks.T, buckets.reshape(tile_shape),
                 desk_owner.reshape(1, desks), block_owner, block_list.T, desk_owner,
             ),
         )
@@ -361,9 +415,6 @@
     moved = {}
     for index in ORDER:
         moved[index] = lax.ppermute(shocks, "fac", pairs[index])
-    device = lax.axis_index("fac")
-    onward = jnp.where((device % 2 == 0) == (device // 2 % 2 == 0), moved[1], moved[2])
-    far = held(lax.ppermute(onward, "fac", pairs[0]))
     chunk_shape = (fac_count, ROWS, LANES)
     coded_shape = pltpu.VMEM((fac_count, 2 * ROWS, LANES // 2), jnp.int16)
     delta, coded, gamma = pl.pallas_call(
@@ -371,34 +422,57 @@
         out_shape=(
             pltpu.VMEM(chunk_shape, f32), coded_shape, pltpu.VMEM(cross_gamma.shape, bf16)
         ),
-        in_specs=[VMEM] * 4 + [HBM],
+        in_specs=[VMEM] * 3 + [HBM] * 2,
         out_specs=(VMEM, VMEM, VMEM),
-        scratch_shapes=[pltpu.SemaphoreType.DMA],
+        scratch_shapes=[pltpu.VMEM((desks, BLK), bf16), pltpu.SemaphoreType.DMA((2,))],
         name="delta",
         compiler_params=limited(16),
-    )(shocks, tiles, sens_t, owner_row, resident(cross_gamma))
+    )(shocks, tiles, owner_row, resident(sensitivity.T), resident(cross_gamma))
+    device = lax.axis_index("fac")
+    onward = jnp.where((device % 2 == 0) == (device // 2 % 2 == 0), moved[1], moved[2])
+    far = held(lax.ppermute(onward, "fac", pairs[0]))
+    nearby, chip_near, chip_far = (held(moved[index]) for index in range(3))
+    product = pl.pallas_call(
+        early_kernel,
+        out_shape=pltpu.VMEM((CAP, HORIZONS * s_dev, BLK), f32),
+        in_specs=[SMEM] + [VMEM] * 6,
+        out_specs=VMEM,
+        name="early",
+        compiler_params=limited(12),
+    )(meta, shocks, nearby, chip_near, chip_far, tiles, gamma)
     terms = pl.pallas_call(
         gamma_kernel,
         out_shape=coded_shape,
-        in_specs=[SMEM] + [VMEM] * 10,
+        in_specs=[SMEM] + [VMEM] * 11,
         out_specs=VMEM,
-        scratch_shapes=[pltpu.VMEM((CAP, ROWS, LANES), f32)],
-        input_output_aliases={10: 0},
+        scratch_shapes=[
+            pltpu.VMEM((CAP, ROWS, LANES), f32),
+            pltpu.VMEM((HORIZONS * s_dev, 1), f32),
+        ],
+        input_output_aliases={11: 0},
         name="gamma",
         compiler_params=limited(16),
-    )(meta, shocks, held(moved[0]), far, held(moved[1]), held(moved[2]), tiles, owner_row, gamma, delta, coded)
+    )(
+        meta, shocks, nearby, far, chip_near, chip_far, tiles, owner_row, gamma, product, delta,
+        coded,
+    )
     received = held(lax.all_to_all(terms, "fac", 0, 0, tiled=False))
-    packed, profit = pl.pallas_call(
+    packed = pl.pallas_call(
         sum_kernel,
-        out_shape=(
-            pltpu.VMEM((HORIZONS * ROWS, 128), f32),
-            jax.ShapeDtypeStruct((DESK_DEV, HORIZONS, s_dev), f32),
-        ),
+        out_shape=pltpu.VMEM((3 * ROWS, 128), f32),
         in_specs=[VMEM],
-        out_specs=(VMEM, VMEM),
+        out_specs=VMEM,
         name="total",
         compiler_params=limited(8),
     )(received)
+    profit = pl.pallas_call(
+        profit_kernel,
+        out_shape=jax.ShapeDtypeStruct((DESK_DEV, HORIZONS, s_dev), f32),
+        in_specs=[VMEM],
+        out_specs=VMEM,
+        name="profit",
+        compiler_params=limited(4),
+    )(packed)
     others = []
     for step in SCEN_ORDER:
         others.append(held(lax.ppermute(packed, "scen", [(i, i ^ step) for i in range(scen_count)])))

time: 52.3 us -> 52 us (level)
  starting transfers between devices: 9.11 us -> 8.18 us
  Pallas kernels: 9.12 us -> 9.66 us
    pallas_call x1 -> x3, Pallas kernels: 0.81 us -> 2.58 us  [the longest x1 1.71 us: local(): pl.pallas_call(early_kernel, out_shape=pltpu.VMEM((CAP, HORIZONS * s_dev,...]
    ppermute x3, starting transfers between devices: 4.76 us -> 3.58 us  [local(): moved[index] = lax.ppermute(shocks, 'fac', pairs[index])]
    pallas_call x1, Pallas kernels: 2.13 us -> 1.19 us  [local(): pl.pallas_call(gamma_kernel, out_shape=coded_shape, in_specs=[SMEM] + [VM...]
  transfers between devices with their start and end apart: 7 -> 7, of which waited for: 4 -> 4; matrix products, arithmetic and copies ran while one was open for 0% -> 0% of each run, Pallas kernels for 5% -> 9%
where the time goes in v5:
time: 52 us; the launch traced here: 51.8 us
  blocking collectives  24.5 us (47%)
  Pallas kernels  9.66 us (19%)
  waiting for transfers between devices  8.62 us (17%)
  starting transfers between devices  8.18 us (16%)
  between operations  0.76 us (1%)
    all_to_all x1, blocking collectives, local(): received = held(lax.all_to_all(terms, 'fac', 0, 0, tiled=False))  24.5 us
    ppermute x3, waiting for transfers between devices, local(): moved[index] = lax.ppermute(shocks, 'fac', pairs[index])  4.82 us
    ppermute x3, starting transfers between devices, local(): lax.ppermute(packed, 'scen', [(i, i ^ step) for i in range(scen_count)])  4.5 us
    ppermute x3, waiting for transfers between devices, local(): lax.ppermute(packed, 'scen', [(i, i ^ step) for i in range(scen_count)])  3.8 us
    ppermute x3, starting transfers between devices, local(): moved[index] = lax.ppermute(shocks, 'fac', pairs[index])  3.58 us
    pallas_call x1, Pallas kernels, local(): pl.pallas_call(delta_kernel, out_shape=(pltpu.VMEM(chunk_shape, f32), cod...  2.4 us
    pallas_call x1, Pallas kernels, local(): pl.pallas_call(shocks_kernel, out_shape=(pltpu.VMEM((s_dev, BLK), bf16),...  2.35 us
    pallas_call x1, Pallas kernels, local(): pl.pallas_call(early_kernel, out_shape=pltpu.VMEM((CAP, HORIZONS * s_dev,...  1.71 us
  transfers between devices with their start and end apart: 7, of which 4 were waited for; matrix products, arithmetic and copies ran while one was open for 0% of the time, Pallas kernels for 9%

profile of v5, /device:TPU:2, one launch (start us, length us, event | category | flops | bytes accessed | tf_op | source)
XLA Modules:
  0.0 51.8 jit_solution(9331033300183302436)
XLA Ops:
  0.6 2.3 %shocks.1 = (bf16[64,1024]{1,0:T(8,128)(2,1)S(1)}, s32[5,8,128]{2,1,0:T(8,128)S(1)}, s32[1,200]{1,0:T(1,128)S(1)}, s32[16]{0:T(128)S(4)}) custom-call(bf16[1000,1024]{1,0:T(8,128)(2,1)} %bitcast.7, bf16[64,1000]{1,0:T(8,128)(2,1)} %bitcast.10, s32[64,8,128]{2,1,0:T(8,128)} %bitcast.9, s32[1,200]{1,0:T(1,128)} %bitcast.11, s32[96]{0:T(128)} %block_owner_hbm.1, ...), custom_call_target="tpu_custom_call" | custom-call | tf_op jit(solution)/shard_map/shocks/pallas_call | solution.py:385
  3.0 3.4 %collective-permute-start.2 = (bf16[64,1024]{1,0:T(8,128)(2,1)S(1)}, bf16[64,1024]{1,0:T(8,128)(2,1)S(1)}, u32[]{:S(2)}, u32[]{:S(2)}) collective-permute-start(bf16[64,1024]{1,0:T(8,128)(2,1)S(1)} %get-tuple-element.13.own), channel_id=1, source_target_pairs={{2,4},{3,5},{4,2},{5,3},{6,8},{7,9},{8,6},{9,7},{10,12},{11,13},{1... | collective-permute-start | bytes 393224 | tf_op jit(solution)/shard_map/ppermute | solution.py:417
  6.4 0.1 collective-permute-start.1
  6.5 0.1 collective-permute-start
  6.6 3.5 %collective-permute-done.2.chip_far = bf16[64,1024]{1,0:T(8,128)(2,1)S(1)} collective-permute-done((bf16[64,1024]{1,0:T(8,128)(2,1)S(1)}, bf16[64,1024]{1,0:T(8,128)(2,1)S(1)}, u32[]{:S(2)}, u32[]{:S(2)}) %collective-permute-start.2) | collective-permute-done | bytes 131104 | tf_op jit(solution)/shard_map/ppermute | solution.py:417
  10.1 1.3 %collective-permute-done.1.chip_near = bf16[64,1024]{1,0:T(8,128)(2,1)S(1)} collective-permute-done((bf16[64,1024]{1,0:T(8,128)(2,1)S(1)}, bf16[64,1024]{1,0:T(8,128)(2,1)S(1)}, u32[]{:S(2)}, u32[]{:S(2)}) %collective-permute-start.1) | collective-permute-done | bytes 131104 | tf_op jit(solution)/shard_map/ppermute | solution.py:417
  11.5 0.1 collective-permute-start.3
  11.6 2.4 %delta.1 = (f32[64,8,256]{2,1,0:T(8,128)S(1)}, s16[64,16,128]{2,1,0:T(8,128)(2,1)S(1)}, bf16[2,1024,1024]{2,1,0:T(8,128)(2,1)S(1)}) custom-call(bf16[64,1024]{1,0:T(8,128)(2,1)S(1)} %get-tuple-element.13.own, s32[5,8,128]{2,1,0:T(8,128)S(1)} %get-tuple-element.14.tiles, s32[1,200]{1,0:T(1,128)S(1)} %get-tuple-element.15.owner_row_ref, ...), custom_call_target="tpu_custom_call" | custom-call | tf_op jit(solution)/shard_map/delta/pallas_call | solution.py:420
  14.0 0.0 collective-permute-done.near
  14.0 1.7 %early.1.product = f32[2,320,1024]{2,1,0:T(8,128)S(1)} custom-call(s32[16]{0:T(128)S(4)} %get-tuple-element.12.meta, bf16[64,1024]{1,0:T(8,128)(2,1)S(1)} %get-tuple-element.13.own, bf16[64,1024]{1,0:T(8,128)(2,1)S(1)} %collective-permute-done.near, bf16[64,1024]{1,0:T(8,128)(2,1)S(1)} %collective-permute-done.1.chip_near, ...), custom_call_target="tpu_custom_call" | custom-call | tf_op jit(solution)/shard_map/early/pallas_call | solution.py:435
  15.7 0.0 collective-permute-done.3.far
  15.7 1.2 %gamma.1 = s16[64,16,128]{2,1,0:T(8,128)(2,1)S(1)} custom-call(s32[16]{0:T(128)S(4)} %get-tuple-element.12.meta, bf16[64,1024]{1,0:T(8,128)(2,1)S(1)} %get-tuple-element.13.own, bf16[64,1024]{1,0:T(8,128)(2,1)S(1)} %collective-permute-done.near, bf16[64,1024]{1,0:T(8,128)(2,1)S(1)} %collective-permute-done.3.far, ...), custom_call_target="tpu_custom_call", output_to_operand_aliasing={{}: (11, {})} | custom-call | tf_op jit(solution)/shard_map/gamma/pallas_call | solution.py:443
  16.9 24.5 %all_to_all.5.received = s16[64,16,128]{2,1,0:T(8,128)(2,1)S(1)} all-to-all(s16[64,16,128]{2,1,0:T(8,128)(2,1)S(1)} %gamma.1), channel_id=1, replica_groups=mesh['scen'=4,'fac'=64] {'fac'}, dimensions={0} | all-to-all | bytes 524288 | tf_op jit(solution)/shard_map/all_to_all | solution.py:459
  41.4 0.2 total.1.packed.own
  41.6 1.6 %collective-permute-start.6 = (f32[24,128]{1,0:T(8,128)S(1)}, f32[24,128]{1,0:T(8,128)S(1)}, u32[]{:S(2)}, u32[]{:S(2)}) collective-permute-start(f32[24,128]{1,0:T(8,128)S(1)} %total.1.packed.own), channel_id=1, source_target_pairs={{0,64},{64,0},{128,192},{192,128},{1,65},{65,1},{129,193},{193,129... | collective-permute-start | bytes 36872 | tf_op jit(solution)/shard_map/ppermute | solution.py:478
  43.2 2.2 %collective-permute-start.5 = (f32[24,128]{1,0:T(8,128)S(1)}, f32[24,128]{1,0:T(8,128)S(1)}, u32[]{:S(2)}, u32[]{:S(2)}) collective-permute-start(f32[24,128]{1,0:T(8,128)S(1)} %total.1.packed.own), channel_id=1, source_target_pairs={{0,192},{64,128},{128,64},{192,0},{1,193},{65,129},{129,65},{193,1... | collective-permute-start | bytes 36872 | tf_op jit(solution)/shard_map/ppermute | solution.py:478
  45.4 0.7 %collective-permute-start.4 = (f32[24,128]{1,0:T(8,128)S(1)}, f32[24,128]{1,0:T(8,128)S(1)}, u32[]{:S(2)}, u32[]{:S(2)}) collective-permute-start(f32[24,128]{1,0:T(8,128)S(1)} %total.1.packed.own), channel_id=1, source_target_pairs={{0,128},{64,192},{128,0},{192,64},{1,129},{65,193},{129,1},{193,65... | collective-permute-start | bytes 36872 | tf_op jit(solution)/shard_map/ppermute | solution.py:478
  46.1 0.7 %profit.1 = f32[5,5,64]{2,1,0:T(8,128)} custom-call(f32[24,128]{1,0:T(8,128)S(1)} %total.1.packed.own), custom_call_target="tpu_custom_call" | custom-call | tf_op jit(solution)/shard_map/profit/pallas_call | solution.py:468
  46.8 0.0 collective-permute-done.6.other3
  46.8 1.3 %collective-permute-done.5.other2 = f32[24,128]{1,0:T(8,128)S(1)} collective-permute-done((f32[24,128]{1,0:T(8,128)S(1)}, f32[24,128]{1,0:T(8,128)S(1)}, u32[]{:S(2)}, u32[]{:S(2)}) %collective-permute-start.5) | collective-permute-done | bytes 12320 | tf_op jit(solution)/shard_map/ppermute | solution.py:478
  48.1 2.5 %collective-permute-done.4.other1 = f32[24,128]{1,0:T(8,128)S(1)} collective-permute-done((f32[24,128]{1,0:T(8,128)S(1)}, f32[24,128]{1,0:T(8,128)S(1)}, u32[]{:S(2)}, u32[]{:S(2)}) %collective-permute-start.4) | collective-permute-done | bytes 12320 | tf_op jit(solution)/shard_map/ppermute | solution.py:478
  50.6 1.1 %tail.1 = (f32[5,5]{1,0:T(8,128)}, f32[1,5]{1,0:T(1,128)}) custom-call(f32[24,128]{1,0:T(8,128)S(1)} %total.1.packed.own, f32[24,128]{1,0:T(8,128)S(1)} %collective-permute-done.4.other1, f32[24,128]{1,0:T(8,128)S(1)} %collective-permute-done.5.other2, f32[24,128]{1,0:T(8,128)S(1)} %collective-permute-done.6.other3), custom_call_target="tpu_custom_call" | custom-call | tf_op jit(solution)/shard_map/tail/pallas_call | solution.py:479
  (1 shorter events, 0.0 us)
Async XLA Ops:
  3.0 7.1 %collective-permute-start.2 = (bf16[64,1024]{1,0:T(8,128)(2,1)S(1)}, bf16[64,1024]{1,0:T(8,128)(2,1)S(1)}, u32[]{:S(2)}, u32[]{:S(2)}) collective-permute-start(bf16[64,1024]{1,0:T(8,128)(2,1)S(1)} %get-tuple-element.13.own), channel_id=1, source_target_pairs={{2,4},{3,5},{4,2},{5,3},{6,8},{7,9},{8,6},{9,7},{10,12},{11,13},{1... | collective-permute-start | bytes 393224 | tf_op jit(solution)/shard_map/ppermute | solution.py:417
  6.4 5.1 %collective-permute-start.1 = (bf16[64,1024]{1,0:T(8,128)(2,1)S(1)}, bf16[64,1024]{1,0:T(8,128)(2,1)S(1)}, u32[]{:S(2)}, u32[]{:S(2)}) collective-permute-start(bf16[64,1024]{1,0:T(8,128)(2,1)S(1)} %get-tuple-element.13.own), channel_id=1, source_target_pairs={{0,2},{1,3},{2,0},{3,1},{4,6},{5,7},{6,4},{7,5},{8,10},{9,11},{10,... | collective-permute-start | bytes 393224 | tf_op jit(solution)/shard_map/ppermute | solution.py:417
  6.5 7.5 %collective-permute-start = (bf16[64,1024]{1,0:T(8,128)(2,1)S(1)}, bf16[64,1024]{1,0:T(8,128)(2,1)S(1)}, u32[]{:S(2)}, u32[]{:S(2)}) collective-permute-start(bf16[64,1024]{1,0:T(8,128)(2,1)S(1)} %get-tuple-element.13.own), channel_id=1, source_target_pairs={{0,1},{1,0},{2,3},{3,2},{4,5},{5,4},{6,7},{7,6},{8,9},{9,8},{10,11... | collective-permute-start | bytes 393224 | tf_op jit(solution)/shard_map/ppermute | solution.py:417
  11.5 4.2 %collective-permute-start.3 = (bf16[64,1024]{1,0:T(8,128)(2,1)S(1)}, bf16[64,1024]{1,0:T(8,128)(2,1)S(1)}, u32[]{:S(2)}, u32[]{:S(2)}) collective-permute-start(bf16[64,1024]{1,0:T(8,128)(2,1)S(1)} %broadcast_select_fusion), channel_id=1, source_target_pairs={{0,1},{1,0},{2,3},{3,2},{4,5},{5,4},{6,7},{7,6},{8,9},{9,8},{10,11... | collective-permute-start | bytes 393224 | tf_op jit(solution)/shard_map/ppermute | solution.py:433
  41.6 5.2 %collective-permute-start.6 = (f32[24,128]{1,0:T(8,128)S(1)}, f32[24,128]{1,0:T(8,128)S(1)}, u32[]{:S(2)}, u32[]{:S(2)}) collective-permute-start(f32[24,128]{1,0:T(8,128)S(1)} %total.1.packed.own), channel_id=1, source_target_pairs={{0,64},{64,0},{128,192},{192,128},{1,65},{65,1},{129,193},{193,129... | collective-permute-start | bytes 36872 | tf_op jit(solution)/shard_map/ppermute | solution.py:478
  43.2 4.9 %collective-permute-start.5 = (f32[24,128]{1,0:T(8,128)S(1)}, f32[24,128]{1,0:T(8,128)S(1)}, u32[]{:S(2)}, u32[]{:S(2)}) collective-permute-start(f32[24,128]{1,0:T(8,128)S(1)} %total.1.packed.own), channel_id=1, source_target_pairs={{0,192},{64,128},{128,64},{192,0},{1,193},{65,129},{129,65},{193,1... | collective-permute-start | bytes 36872 | tf_op jit(solution)/shard_map/ppermute | solution.py:478
  45.4 5.2 %collective-permute-start.4 = (f32[24,128]{1,0:T(8,128)S(1)}, f32[24,128]{1,0:T(8,128)S(1)}, u32[]{:S(2)}, u32[]{:S(2)}) collective-permute-start(f32[24,128]{1,0:T(8,128)S(1)} %total.1.packed.own), channel_id=1, source_target_pairs={{0,128},{64,192},{128,0},{192,64},{1,129},{65,193},{129,1},{193,65... | collective-permute-start | bytes 36872 | tf_op jit(solution)/shard_map/ppermute | solution.py:478

commit v6 on v5

--- a/solution.py
+++ b/solution.py
@@ -12,7 +12,7 @@
 ROWS = 8
 LANES = 256
 TAIL = 7
-CHUNKS = 4
+CHUNKS = 2
 FAR = 2
 
 horizon_weights = (1.0, 1.0, 2.0, 2.0, 6.0)
@@ -132,7 +132,7 @@
 
 
 def delta_kernel(
-    own, tiles, owner_row_ref, sens_hbm, gamma_hbm, out, coded, gamma, sens_t, sems
+    meta, own, tiles, owner_row_ref, sens_hbm, gamma_hbm, out, coded, gamma, ranks, sens_t, sems
 ):
     sens_copy = pltpu.make_async_copy(sens_hbm, sens_t, sems.at[0])
     copy = pltpu.make_async_copy(gamma_hbm, gamma, sems.at[1])
@@ -174,6 +174,13 @@
     chunks = packed.reshape(fac_count, ROWS, LANES)
     out[...] = chunks
     coded[...] = encoded(chunks)
+    for slot in range(CAP):
+        earlier = jnp.logical_and(
+            owner_row == meta[6 + 6 * slot],
+            lax.broadcasted_iota(jnp.int32, (1, desks), 1) < meta[5 + 6 * slot],
+        )
+        found = jnp.sum(jnp.where(earlier, 1.0, 0.0), axis=1, keepdims=True).astype(jnp.int32)
+        ranks[slot] = jnp.broadcast_to(found, (ROWS, 128))
     copy.wait()
 
 
@@ -209,80 +216,57 @@
 
 
 def gamma_kernel(
-    meta, own, near, far, chip_near, chip_far, tiles, owner_row_ref, gamma, product, delta, coded,
-    out, sums, quads,
+    meta, own, near, far, chip_near, chip_far, tiles, ranks, gamma, early, delta, coded,
+    out, product,
 ):
-    del coded
-    desks = owner_row_ref.shape[1]
+    del coded, early
     width = HORIZONS * own.shape[0]
     live = meta[0]
-    sums[...] = jnp.zeros(sums.shape, jnp.float32)
     others = ((1, near), (FAR, far), (3, chip_near), (4, chip_far))
-
     for slot in range(CAP):
-        @pl.when(slot < live)
+        both = jnp.logical_and(meta[2 + 6 * slot] == FAR, meta[4 + 6 * slot] == FAR)
+
+        @pl.when(jnp.logical_and(slot < live, both))
         def _(slot=slot):
-            row_code = meta[2 + 6 * slot]
-            col_code = meta[4 + 6 * slot]
-            desk = meta[5 + 6 * slot]
-            owner = meta[6 + 6 * slot]
-            use_row = row_code == FAR
-            tile = jnp.where(use_row, tiles[1 + 2 * slot], tiles[2 + 2 * slot])
-            part = picked(jnp.where(use_row, row_code, col_code), tile, own, others)
-            whole = part.astype(jnp.float32)
-            both = jnp.logical_and(use_row, col_code == FAR)
-
-            @pl.when(both)
-            def _():
-                value = lax.dot_general(
-                    part, gamma[slot], (((1,), (0,)), ((), ())), preferred_element_type=jnp.float32
-                )
-                quads[...] = jnp.sum(whole * value, axis=1, keepdims=True)
-
-            @pl.when(jnp.logical_not(both))
-            def _():
-                quads[...] = jnp.sum(whole * product[slot], axis=1, keepdims=True)
-
-            quad = 0.5 * quads[...]
-            diagonal = lax.broadcasted_iota(jnp.int32, (width, width), 0) == lax.broadcasted_iota(
-                jnp.int32, (width, width), 1
+            part = masked_rows(far[...], tiles[1 + 2 * slot])
+            product[slot] = lax.dot_general(
+                part, gamma[slot], (((1,), (0,)), ((), ())), preferred_element_type=jnp.float32
             )
-            quad_row = jnp.sum(
-                jnp.where(diagonal, jnp.broadcast_to(quad, (width, width)), 0.0),
-                axis=0,
-                keepdims=True,
-            )
-            earlier = jnp.logical_and(
-                owner_row_ref[...] == owner, lax.broadcasted_iota(jnp.int32, (1, desks), 1) < desk
-            )
-            rank = jnp.sum(jnp.where(earlier, 1.0, 0.0), axis=1, keepdims=True).astype(jnp.int32)
-            rank = jnp.broadcast_to(rank, (ROWS, LANES))
-            tail_row = jnp.concatenate([quad_row[:, LANES:]] * 4, axis=1)
-            quarter = lax.broadcasted_iota(jnp.int32, (ROWS, LANES), 1) // 64
-            row = lax.broadcasted_iota(jnp.int32, (ROWS, LANES), 0)
-            moved = jnp.where(rank >= 4, 4, 0)
-            in_tail = jnp.logical_and(
-                row == DESK_DEV + jnp.where(rank >= 4, 1, 0), quarter == rank - moved
-            )
-            sums[slot] = jnp.where(
-                row == rank,
-                jnp.broadcast_to(quad_row[:, :LANES], (ROWS, LANES)),
-                jnp.where(in_tail, jnp.broadcast_to(tail_row, (ROWS, LANES)), 0.0),
-            )
-
+
+    diagonal = lax.broadcasted_iota(jnp.int32, (width, width), 0) == lax.broadcasted_iota(
+        jnp.int32, (width, width), 1
+    )
+    quarter = lax.broadcasted_iota(jnp.int32, (ROWS, LANES), 1) // 64
+    row = lax.broadcasted_iota(jnp.int32, (ROWS, LANES), 0)
+    sums = []
+    for slot in range(CAP):
+        row_code = meta[2 + 6 * slot]
+        use_row = row_code == FAR
+        tile = jnp.where(use_row, tiles[1 + 2 * slot], tiles[2 + 2 * slot])
+        part = picked(jnp.where(use_row, row_code, meta[4 + 6 * slot]), tile, own, others)
+        quad = 0.5 * jnp.sum(part.astype(jnp.float32) * product[slot], axis=1, keepdims=True)
+        quad_row = jnp.sum(
+            jnp.where(diagonal, jnp.broadcast_to(quad, (width, width)), 0.0), axis=0, keepdims=True
+        )
+        rank = jnp.concatenate([ranks[slot]] * 2, axis=1)
+        tail_row = jnp.concatenate([quad_row[:, LANES:]] * 4, axis=1)
+        moved = jnp.where(rank >= 4, 4, 0)
+        in_tail = jnp.logical_and(
+            row == DESK_DEV + jnp.where(rank >= 4, 1, 0), quarter == rank - moved
+        )
+        addend = jnp.where(
+            row == rank,
+            jnp.broadcast_to(quad_row[:, :LANES], (ROWS, LANES)),
+            jnp.where(in_tail, jnp.broadcast_to(tail_row, (ROWS, LANES)), 0.0),
+        )
+        sums.append(jnp.where(slot < live, addend, 0.0))
     first = meta[6]
     second = jnp.where(live > 1, meta[12], first)
-    joint = jnp.where(first == second, 1.0, 0.0)
-
-    @pl.when(live > 0)
-    def _():
-        one = delta[first] + sums[0] + joint * sums[1]
-        out[first] = encoded(one[None])[0]
-
-    @pl.when(live > 1)
-    def _():
-        two = delta[second] + sums[1] + joint * sums[0]
-        out[second] = encoded(two[None])[0]
+    same = first == second
+    one = delta[first] + sums[0] + jnp.where(same, sums[1], 0.0)
+    two = delta[second] + sums[1] + jnp.where(same, sums[0], 0.0)
+    out[first] = encoded(one[None])[0]
+    out[second] = encoded(two[None])[0]
 
 
 def sum_kernel(received, packed):
@@ -417,43 +401,41 @@
         moved[index] = lax.ppermute(shocks, "fac", pairs[index])
     chunk_shape = (fac_count, ROWS, LANES)
     coded_shape = pltpu.VMEM((fac_count, 2 * ROWS, LANES // 2), jnp.int16)
-    delta, coded, gamma = pl.pallas_call(
+    delta, coded, gamma, ranks = pl.pallas_call(
         delta_kernel,
         out_shape=(
-            pltpu.VMEM(chunk_shape, f32), coded_shape, pltpu.VMEM(cross_gamma.shape, bf16)
+            pltpu.VMEM(chunk_shape, f32), coded_shape, pltpu.VMEM(cross_gamma.shape, bf16),
+            pltpu.VMEM((CAP, ROWS, 128), i32),
         ),
-        in_specs=[VMEM] * 3 + [HBM] * 2,
-        out_specs=(VMEM, VMEM, VMEM),
+        in_specs=[SMEM] + [VMEM] * 3 + [HBM] * 2,
+        out_specs=(VMEM, VMEM, VMEM, VMEM),
         scratch_shapes=[pltpu.VMEM((desks, BLK), bf16), pltpu.SemaphoreType.DMA((2,))],
         name="delta",
         compiler_params=limited(16),
-    )(shocks, tiles, owner_row, resident(sensitivity.T), resident(cross_gamma))
+    )(meta, shocks, tiles, owner_row, resident(sensitivity.T), resident(cross_gamma))
     device = lax.axis_index("fac")
     onward = jnp.where((device % 2 == 0) == (device // 2 % 2 == 0), moved[1], moved[2])
     far = held(lax.ppermute(onward, "fac", pairs[0]))
     nearby, chip_near, chip_far = (held(moved[index]) for index in range(3))
+    product_shape = pltpu.VMEM((CAP, HORIZONS * s_dev, BLK), f32)
     product = pl.pallas_call(
         early_kernel,
-        out_shape=pltpu.VMEM((CAP, HORIZONS * s_dev, BLK), f32),
+        out_shape=product_shape,
         in_specs=[SMEM] + [VMEM] * 6,
         out_specs=VMEM,
         name="early",
         compiler_params=limited(12),
     )(meta, shocks, nearby, chip_near, chip_far, tiles, gamma)
-    terms = pl.pallas_call(
+    terms, _ = pl.pallas_call(
         gamma_kernel,
-        out_shape=coded_shape,
+        out_shape=(coded_shape, product_shape),
         in_specs=[SMEM] + [VMEM] * 11,
-        out_specs=VMEM,
-        scratch_shapes=[
-            pltpu.VMEM((CAP, ROWS, LANES), f32),
-            pltpu.VMEM((HORIZONS * s_dev, 1), f32),
-        ],
-        input_output_aliases={11: 0},
+        out_specs=(VMEM, VMEM),
+        input_output_aliases={11: 0, 9: 1},
         name="gamma",
         compiler_params=limited(16),
     )(
-        meta, shocks, nearby, far, chip_near, chip_far, tiles, owner_row, gamma, product, delta,
+        meta, shocks, nearby, far, chip_near, chip_far, tiles, ranks, gamma, product, delta,
         coded,
     )
     received = held(lax.all_to_all(terms, "fac", 0, 0, tiled=False))

time: 52 us -> 51.1 us (0.983)
  Pallas kernels: 9.66 us -> 8.72 us
    pallas_call x2, Pallas kernels: 2.9 us -> 2.27 us  [the longest x1 1.72 us: local(): pl.pallas_call(early_kernel, out_shape=product_shape, in_specs=[SMEM] + [...]
where the time goes in v6:
time: 51.1 us; the launch traced here: 50.8 us
  blocking collectives  24.5 us (48%)
  Pallas kernels  8.72 us (17%)
  waiting for transfers between devices  8.62 us (17%)
  starting transfers between devices  8.18 us (16%)
  between operations  0.76 us (1%)
    all_to_all x1, blocking collectives, local(): received = held(lax.all_to_all(terms, 'fac', 0, 0, tiled=False))  24.5 us
    ppermute x3, waiting for transfers between devices, local(): moved[index] = lax.ppermute(shocks, 'fac', pairs[index])  4.82 us
    ppermute x3, starting transfers between devices, local(): lax.ppermute(packed, 'scen', [(i, i ^ step) for i in range(scen_count)])  4.5 us
    ppermute x3, waiting for transfers between devices, local(): lax.ppermute(packed, 'scen', [(i, i ^ step) for i in range(scen_count)])  3.8 us
    ppermute x3, starting transfers between devices, local(): moved[index] = lax.ppermute(shocks, 'fac', pairs[index])  3.59 us
    pallas_call x1, Pallas kernels, local(): pl.pallas_call(delta_kernel, out_shape=(pltpu.VMEM(chunk_shape, f32), cod...  2.41 us
    pallas_call x1, Pallas kernels, local(): pl.pallas_call(shocks_kernel, out_shape=(pltpu.VMEM((s_dev, BLK), bf16),...  2.02 us
    pallas_call x1, Pallas kernels, local(): pl.pallas_call(early_kernel, out_shape=product_shape, in_specs=[SMEM] + [...  1.72 us
  transfers between devices with their start and end apart: 7, of which 4 were waited for; matrix products, arithmetic and copies ran while one was open for 0% of the time, Pallas kernels for 9%

profile of v6, /device:TPU:2, one launch (start us, length us, event | category | flops | bytes accessed | tf_op | source)
XLA Modules:
  0.0 50.8 jit_solution(17077308183414573858)
XLA Ops:
  0.6 2.0 %shocks.1 = (bf16[64,1024]{1,0:T(8,128)(2,1)S(1)}, s32[5,8,128]{2,1,0:T(8,128)S(1)}, s32[1,200]{1,0:T(1,128)S(1)}, s32[16]{0:T(128)S(4)}) custom-call(bf16[1000,1024]{1,0:T(8,128)(2,1)} %bitcast.7, bf16[64,1000]{1,0:T(8,128)(2,1)} %bitcast.10, s32[64,8,128]{2,1,0:T(8,128)} %bitcast.9, s32[1,200]{1,0:T(1,128)} %bitcast.11, s32[96]{0:T(128)} %block_owner_hbm.1, ...), custom_call_target="tpu_custom_call" | custom-call | tf_op jit(solution)/shard_map/shocks/pallas_call | solution.py:369
  2.7 3.4 %collective-permute-start.2 = (bf16[64,1024]{1,0:T(8,128)(2,1)S(1)}, bf16[64,1024]{1,0:T(8,128)(2,1)S(1)}, u32[]{:S(2)}, u32[]{:S(2)}) collective-permute-start(bf16[64,1024]{1,0:T(8,128)(2,1)S(1)} %get-tuple-element.15.own), channel_id=1, source_target_pairs={{2,4},{3,5},{4,2},{5,3},{6,8},{7,9},{8,6},{9,7},{10,12},{11,13},{1... | collective-permute-start | bytes 393224 | tf_op jit(solution)/shard_map/ppermute | solution.py:401
  6.1 0.1 collective-permute-start.1
  6.2 0.1 collective-permute-start
  6.3 3.5 %collective-permute-done.2.chip_far = bf16[64,1024]{1,0:T(8,128)(2,1)S(1)} collective-permute-done((bf16[64,1024]{1,0:T(8,128)(2,1)S(1)}, bf16[64,1024]{1,0:T(8,128)(2,1)S(1)}, u32[]{:S(2)}, u32[]{:S(2)}) %collective-permute-start.2) | collective-permute-done | bytes 131104 | tf_op jit(solution)/shard_map/ppermute | solution.py:401
  9.8 1.3 %collective-permute-done.1.chip_near = bf16[64,1024]{1,0:T(8,128)(2,1)S(1)} collective-permute-done((bf16[64,1024]{1,0:T(8,128)(2,1)S(1)}, bf16[64,1024]{1,0:T(8,128)(2,1)S(1)}, u32[]{:S(2)}, u32[]{:S(2)}) %collective-permute-start.1) | collective-permute-done | bytes 131104 | tf_op jit(solution)/shard_map/ppermute | solution.py:401
  11.1 0.1 collective-permute-start.3
  11.2 2.4 %delta.1 = (f32[64,8,256]{2,1,0:T(8,128)S(1)}, s16[64,16,128]{2,1,0:T(8,128)(2,1)S(1)}, bf16[2,1024,1024]{2,1,0:T(8,128)(2,1)S(1)}, s32[2,8,128]{2,1,0:T(8,128)S(1)}) custom-call(s32[16]{0:T(128)S(4)} %get-tuple-element.14.meta, bf16[64,1024]{1,0:T(8,128)(2,1)S(1)} %get-tuple-element.15.own, s32[5,8,128]{2,1,0:T(8,128)S(1)} %get-tuple-element.16.tiles, ...), custom_call_target="tpu_custom_call" | custom-call | tf_op jit(solution)/shard_map/delta/pallas_call | solution.py:404
  13.7 0.0 collective-permute-done.near
  13.7 1.7 %early.1 = f32[2,320,1024]{2,1,0:T(8,128)S(1)} custom-call(s32[16]{0:T(128)S(4)} %get-tuple-element.14.meta, bf16[64,1024]{1,0:T(8,128)(2,1)S(1)} %get-tuple-element.15.own, bf16[64,1024]{1,0:T(8,128)(2,1)S(1)} %collective-permute-done.near, bf16[64,1024]{1,0:T(8,128)(2,1)S(1)} %collective-permute-done.1.chip_near, ...), custom_call_target="tpu_custom_call" | custom-call | tf_op jit(solution)/shard_map/early/pallas_call | solution.py:421
  15.4 0.0 collective-permute-done.3.far
  15.4 0.5 %gamma.1 = (s16[64,16,128]{2,1,0:T(8,128)(2,1)S(1)}, f32[2,320,1024]{2,1,0:T(8,128)S(1)}) custom-call(s32[16]{0:T(128)S(4)} %get-tuple-element.14.meta, bf16[64,1024]{1,0:T(8,128)(2,1)S(1)} %get-tuple-element.15.own, bf16[64,1024]{1,0:T(8,128)(2,1)S(1)} %collective-permute-done.near, ...), custom_call_target="tpu_custom_call", output_to_operand_aliasing={{0}: (11, {}), {1}: (9, {})} | custom-call | tf_op jit(solution)/shard_map/gamma/pallas_call | solution.py:429
  16.0 24.5 %all_to_all.5.received = s16[64,16,128]{2,1,0:T(8,128)(2,1)S(1)} all-to-all(s16[64,16,128]{2,1,0:T(8,128)(2,1)S(1)} %get-tuple-element.22), channel_id=1, replica_groups=mesh['scen'=4,'fac'=64] {'fac'}, dimensions={0} | all-to-all | bytes 524288 | tf_op jit(solution)/shard_map/all_to_all | solution.py:441
  40.5 0.2 total.1.packed.own
  40.7 1.6 %collective-permute-start.6 = (f32[24,128]{1,0:T(8,128)S(1)}, f32[24,128]{1,0:T(8,128)S(1)}, u32[]{:S(2)}, u32[]{:S(2)}) collective-permute-start(f32[24,128]{1,0:T(8,128)S(1)} %total.1.packed.own), channel_id=1, source_target_pairs={{0,64},{64,0},{128,192},{192,128},{1,65},{65,1},{129,193},{193,129... | collective-permute-start | bytes 36872 | tf_op jit(solution)/shard_map/ppermute | solution.py:460
  42.3 2.2 %collective-permute-start.5 = (f32[24,128]{1,0:T(8,128)S(1)}, f32[24,128]{1,0:T(8,128)S(1)}, u32[]{:S(2)}, u32[]{:S(2)}) collective-permute-start(f32[24,128]{1,0:T(8,128)S(1)} %total.1.packed.own), channel_id=1, source_target_pairs={{0,192},{64,128},{128,64},{192,0},{1,193},{65,129},{129,65},{193,1... | collective-permute-start | bytes 36872 | tf_op jit(solution)/shard_map/ppermute | solution.py:460
  44.5 0.7 %collective-permute-start.4 = (f32[24,128]{1,0:T(8,128)S(1)}, f32[24,128]{1,0:T(8,128)S(1)}, u32[]{:S(2)}, u32[]{:S(2)}) collective-permute-start(f32[24,128]{1,0:T(8,128)S(1)} %total.1.packed.own), channel_id=1, source_target_pairs={{0,128},{64,192},{128,0},{192,64},{1,129},{65,193},{129,1},{193,65... | collective-permute-start | bytes 36872 | tf_op jit(solution)/shard_map/ppermute | solution.py:460
  45.2 0.7 %profit.1 = f32[5,5,64]{2,1,0:T(8,128)} custom-call(f32[24,128]{1,0:T(8,128)S(1)} %total.1.packed.own), custom_call_target="tpu_custom_call" | custom-call | tf_op jit(solution)/shard_map/profit/pallas_call | solution.py:450
  45.9 0.0 collective-permute-done.6.other3
  45.9 1.3 %collective-permute-done.5.other2 = f32[24,128]{1,0:T(8,128)S(1)} collective-permute-done((f32[24,128]{1,0:T(8,128)S(1)}, f32[24,128]{1,0:T(8,128)S(1)}, u32[]{:S(2)}, u32[]{:S(2)}) %collective-permute-start.5) | collective-permute-done | bytes 12320 | tf_op jit(solution)/shard_map/ppermute | solution.py:460
  47.2 2.5 %collective-permute-done.4.other1 = f32[24,128]{1,0:T(8,128)S(1)} collective-permute-done((f32[24,128]{1,0:T(8,128)S(1)}, f32[24,128]{1,0:T(8,128)S(1)}, u32[]{:S(2)}, u32[]{:S(2)}) %collective-permute-start.4) | collective-permute-done | bytes 12320 | tf_op jit(solution)/shard_map/ppermute | solution.py:460
  49.7 1.1 %tail.1 = (f32[5,5]{1,0:T(8,128)}, f32[1,5]{1,0:T(1,128)}) custom-call(f32[24,128]{1,0:T(8,128)S(1)} %total.1.packed.own, f32[24,128]{1,0:T(8,128)S(1)} %collective-permute-done.4.other1, f32[24,128]{1,0:T(8,128)S(1)} %collective-permute-done.5.other2, f32[24,128]{1,0:T(8,128)S(1)} %collective-permute-done.6.other3), custom_call_target="tpu_custom_call" | custom-call | tf_op jit(solution)/shard_map/tail/pallas_call | solution.py:461
  (1 shorter events, 0.0 us)
Async XLA Ops:
  2.7 7.1 %collective-permute-start.2 = (bf16[64,1024]{1,0:T(8,128)(2,1)S(1)}, bf16[64,1024]{1,0:T(8,128)(2,1)S(1)}, u32[]{:S(2)}, u32[]{:S(2)}) collective-permute-start(bf16[64,1024]{1,0:T(8,128)(2,1)S(1)} %get-tuple-element.15.own), channel_id=1, source_target_pairs={{2,4},{3,5},{4,2},{5,3},{6,8},{7,9},{8,6},{9,7},{10,12},{11,13},{1... | collective-permute-start | bytes 393224 | tf_op jit(solution)/shard_map/ppermute | solution.py:401
  6.1 5.1 %collective-permute-start.1 = (bf16[64,1024]{1,0:T(8,128)(2,1)S(1)}, bf16[64,1024]{1,0:T(8,128)(2,1)S(1)}, u32[]{:S(2)}, u32[]{:S(2)}) collective-permute-start(bf16[64,1024]{1,0:T(8,128)(2,1)S(1)} %get-tuple-element.15.own), channel_id=1, source_target_pairs={{0,2},{1,3},{2,0},{3,1},{4,6},{5,7},{6,4},{7,5},{8,10},{9,11},{10,... | collective-permute-start | bytes 393224 | tf_op jit(solution)/shard_map/ppermute | solution.py:401
  6.2 7.5 %collective-permute-start = (bf16[64,1024]{1,0:T(8,128)(2,1)S(1)}, bf16[64,1024]{1,0:T(8,128)(2,1)S(1)}, u32[]{:S(2)}, u32[]{:S(2)}) collective-permute-start(bf16[64,1024]{1,0:T(8,128)(2,1)S(1)} %get-tuple-element.15.own), channel_id=1, source_target_pairs={{0,1},{1,0},{2,3},{3,2},{4,5},{5,4},{6,7},{7,6},{8,9},{9,8},{10,11... | collective-permute-start | bytes 393224 | tf_op jit(solution)/shard_map/ppermute | solution.py:401
  11.1 4.3 %collective-permute-start.3 = (bf16[64,1024]{1,0:T(8,128)(2,1)S(1)}, bf16[64,1024]{1,0:T(8,128)(2,1)S(1)}, u32[]{:S(2)}, u32[]{:S(2)}) collective-permute-start(bf16[64,1024]{1,0:T(8,128)(2,1)S(1)} %broadcast_select_fusion), channel_id=1, source_target_pairs={{0,1},{1,0},{2,3},{3,2},{4,5},{5,4},{6,7},{7,6},{8,9},{9,8},{10,11... | collective-permute-start | bytes 393224 | tf_op jit(solution)/shard_map/ppermute | solution.py:418
  40.7 5.2 %collective-permute-start.6 = (f32[24,128]{1,0:T(8,128)S(1)}, f32[24,128]{1,0:T(8,128)S(1)}, u32[]{:S(2)}, u32[]{:S(2)}) collective-permute-start(f32[24,128]{1,0:T(8,128)S(1)} %total.1.packed.own), channel_id=1, source_target_pairs={{0,64},{64,0},{128,192},{192,128},{1,65},{65,1},{129,193},{193,129... | collective-permute-start | bytes 36872 | tf_op jit(solution)/shard_map/ppermute | solution.py:460
  42.3 4.9 %collective-permute-start.5 = (f32[24,128]{1,0:T(8,128)S(1)}, f32[24,128]{1,0:T(8,128)S(1)}, u32[]{:S(2)}, u32[]{:S(2)}) collective-permute-start(f32[24,128]{1,0:T(8,128)S(1)} %total.1.packed.own), channel_id=1, source_target_pairs={{0,192},{64,128},{128,64},{192,0},{1,193},{65,129},{129,65},{193,1... | collective-permute-start | bytes 36872 | tf_op jit(solution)/shard_map/ppermute | solution.py:460
  44.5 5.2 %collective-permute-start.4 = (f32[24,128]{1,0:T(8,128)S(1)}, f32[24,128]{1,0:T(8,128)S(1)}, u32[]{:S(2)}, u32[]{:S(2)}) collective-permute-start(f32[24,128]{1,0:T(8,128)S(1)} %total.1.packed.own), channel_id=1, source_target_pairs={{0,128},{64,192},{128,0},{192,64},{1,129},{65,193},{129,1},{193,65... | collective-permute-start | bytes 36872 | tf_op jit(solution)/shard_map/ppermute | solution.py:460
